TPU v7x, 32 devices: a whole 2x2x4 slice. The times are simulated.
32 devices in a mesh: grp: 2 (over x), path: 8 (over z, y), state: 2 (over core).
Axes of the slice: x: 2, y: 2, z: 4, core: 2. Of those that a mesh axis runs over, the one named last changes fastest.
Arguments:
- start_states: bfloat16 [2, 2, 128, 128, 128], P(None, 'state', 'path'), may hold values from -6 to 6
- block_gates: bfloat16 [3, 2, 128, 128], replicated, may hold values from -0.5 to 0.5
- cut_ops: float32 [2, 6, 2, 2, 2], replicated, may hold values from -4 to 4
- path_bits: int32 [16, 6], P(('grp', 'path')), parts along dimension 0, may hold values from 0 to 1
- left_pick: int32 [8], replicated, may hold values from 0 to 4194303
- right_pick: int32 [8], replicated, may hold values from 0 to 4194303
Outputs:
- amp_left: float32 [16, 2, 128, 128, 128], P('grp', 'state', 'path'), parts along dimension 0
- amp_right: float32 [16, 2, 128, 128, 128], P('grp', 'state', 'path'), parts along dimension 0
There are 2 independent parts, one for each index of `grp`. A program takes and returns all parts, laid end to end along the dimension named above; an argument that names none is the same for every part. Nothing has to cross between parts.
All inputs are finite; a program needn't handle non-finite values.
Results may differ from a plain program's by a relative error of at most 0.0085.
Values may be sent and summed in bfloat16 or wider, within the bound.
A program may use at most 128 MiB of HBM per device.

v0:
```python
import math

import jax
import jax.numpy as jnp
from jax import lax
from jax.sharding import PartitionSpec as P


def cut_kernel(cut_pair, bit_row, dimension):
    result = jnp.eye(dimension // 2 ** bit_row.shape[0], dtype=jnp.float32)
    for position in reversed(range(bit_row.shape[0])):
        picked = jnp.where(bit_row[position] == 1, cut_pair[position, 1], cut_pair[position, 0])
        result = jnp.kron(result, picked)
    return result


def mixed_pair(gate_pair, cuts_pair, bit_row):
    dimension = gate_pair.shape[-1]
    mixed = [
        jnp.dot(
            gate_pair[which_half].astype(jnp.float32),
            cut_kernel(cuts_pair[which_half], bit_row, dimension),
            precision=lax.Precision.HIGHEST,
        )
        for which_half in range(2)
    ]
    return jnp.stack(mixed).astype(jnp.bfloat16)


def apply_last(matrices, states):
    return jnp.einsum(
        "h...j,hij->h...i", states, matrices, preferred_element_type=jnp.float32
    ).astype(jnp.bfloat16)


def apply_middle(matrices, states):
    return jnp.einsum(
        "hxjz,hij->hxiz", states, matrices, preferred_element_type=jnp.float32
    ).astype(jnp.bfloat16)


def order_rows(matrices, owners):
    dimension = matrices.shape[-1]
    split = matrices.reshape(2, 2, owners, dimension // (2 * owners), dimension)
    return jnp.transpose(split, (0, 2, 1, 3, 4)).reshape(2, dimension, dimension)


def top_block(states, matrices):
    dimension = states.shape[-1]
    shaped = states.reshape(2, 1, dimension // 2, 2, dimension, dimension)
    received = lax.all_to_all(shaped, "state", split_axis=3, concat_axis=1, tiled=True)
    columns = received.shape[-1]
    merged = received.reshape(2, dimension, dimension * columns)
    turned = jnp.einsum("hiw,hwc->hic", matrices, merged, preferred_element_type=jnp.float32)
    return turned.astype(jnp.bfloat16).reshape(2, dimension, dimension, columns)


def third_block(first_state, block_gates, cut_ops, bit_row, sections):
    matrices = mixed_pair(block_gates[2], cut_ops[:, sections:], bit_row[sections:])
    return top_block(first_state, order_rows(matrices, lax.axis_size("path")))


def run_paths(base_state, block_gates, cut_ops, path_bits, sections):

    def one_path(bit_row):
        first_state = apply_middle(
            mixed_pair(block_gates[1], cut_ops[:, :sections], bit_row[:sections]), base_state
        )
        return third_block(first_state, block_gates, cut_ops, bit_row, sections)

    return lax.map(one_path, path_bits)


def pick_direct(finals, picks, which_half, owner_index, owners):
    dimension = finals.shape[-1]
    half_block = dimension // (2 * owners)
    flattened = finals[:, which_half].reshape(finals.shape[0], dimension**3)
    top_bit = picks // dimension**3
    row_index = picks // (dimension * dimension) % dimension
    rest = picks % (dimension * dimension)
    high_row = row_index // 2
    local_row = (
        high_row // half_block * (2 * half_block) + top_bit * half_block + high_row % half_block
    )
    values = jnp.take(flattened, local_row * dimension * dimension + rest, axis=1)
    return jnp.where((row_index % 2 == owner_index)[None, :], values, jnp.zeros_like(values))


def body(start_states, block_gates, cut_ops, path_bits, left_pick, right_pick):
    sections = path_bits.shape[1] // 2
    base_state = apply_last(
        block_gates[0], lax.all_gather(start_states, "path", axis=2, tiled=True)
    )[:, 0]
    finals = run_paths(base_state, block_gates, cut_ops, path_bits, sections)
    owner_index = lax.axis_index("state")
    owners = lax.axis_size("path")
    chosen = jnp.stack(
        [
            pick_direct(finals, left_pick, 0, owner_index, owners),
            pick_direct(finals, right_pick, 1, owner_index, owners),
        ],
        axis=1,
    )
    pooled = lax.all_gather(chosen, ("path", "state"), axis=0, tiled=True)
    per_device = chosen.shape[0]
    selected = chosen.shape[-1]
    pooled = pooled.reshape(-1, lax.axis_size("state"), per_device, 2, selected)
    merged = (
        jnp.sum(pooled.astype(jnp.float32), axis=1).astype(jnp.bfloat16).reshape(-1, 2, selected)
    )
    left_vals = merged[:, 0]
    right_vals = merged[:, 1]
    norm_scale = 1.0 / math.sqrt(merged.shape[0])
    dimension = finals.shape[-1]
    half_block = dimension // (2 * owners)
    left_split = left_vals.reshape(owners, per_device, selected)
    right_split = right_vals.reshape(owners, per_device, selected)
    shaped = finals.reshape(per_device, 2, 2 * owners, half_block, dimension, dimension)
    received = lax.all_to_all(shaped, ("path", "state"), split_axis=2, concat_axis=0, tiled=True)
    columns = received.shape[-1]
    parts = received.reshape(owners, 2, per_device, 2, half_block, dimension, columns)
    amp_left = (
        jnp.einsum(
            "pqj,puqkyz->jkuyz", right_split, parts[:, :, :, 0], preferred_element_type=jnp.float32
        )
        * norm_scale
    )
    amp_right = (
        jnp.einsum(
            "pqj,puqkyz->jkuyz", left_split, parts[:, :, :, 1], preferred_element_type=jnp.float32
        )
        * norm_scale
    )
    out_shape = (selected, 2 * half_block, dimension, columns)
    amp_left, amp_right = (amp_left.reshape(out_shape), amp_right.reshape(out_shape))
    return (amp_left[:, None], amp_right[:, None])


def solution(mesh):
    in_specs = (P(None, "state", "path", None, None), P(), P(), P(("grp", "path"), None), P(), P())
    out_specs = (P("grp", "state", "path", None, None), P("grp", "state", "path", None, None))
    return jax.shard_map(body, mesh=mesh, in_specs=in_specs, out_specs=out_specs, check_vma=False)
```

profile of v0, /device:TPU:9, one launch (start us, length us, event | category | flops | bytes accessed | tf_op | source)
XLA Modules:
  0.0 440.9 jit_solution(17451517022726358403)
XLA Ops:
  7.2 0.7 all-gather.2.cloned.1.call-update
  7.9 1.5 fusion.58
  13.3 0.8 slice_bitcast_fusion.1
  15.0 0.6 mul.411
  15.6 2.4 broadcast_multiply_fusion.1
  18.0 4.2 mul.415
  22.6 0.6 mul.422
  23.3 2.4 broadcast_multiply_fusion
  25.7 4.0 mul.426
  30.7 2.4 broadcast_multiply_fusion.3
  33.1 4.0 mul.393
  38.2 2.4 broadcast_multiply_fusion.2
  40.6 4.0 mul.404
  45.5 87.7 %all-gather.2.cloned.1.call-done = bf16[2,1,128,128,128]{4,3,2,0,1:T(8,128)(2,1)} async-done(((bf16[2,1,16,128,128]{4,3,2,0,1:T(8,128)(2,1)}), bf16[2,1,128,128,128]{4,3,2,0,1:T(8,128)(2,1)}) %all-gather.2.cloned.1.call-update) | async-done | bytes 8388624 | tf_op jit(solution)/shard_map/all_gather | solution.py:92
  133.2 9.2 %fusion.8 = bf16[2,128,128,128]{3,1,2,0:T(8,128)(2,1)} fusion(bf16[2,1,128,128,128]{4,3,2,0,1:T(8,128)(2,1)} %all-gather.2.cloned.1.call-done, bf16[1,128,128]{1,2,0:T(8,128)(2,1)S(1)} %fusion.16, bf16[1,128,128]{1,2,0:T(8,128)(2,1)S(1)} %fusion.15, bf16[3,2,128,128]{3,2,1,0:T(8,128)(2,1)S(1)} %copy-done), kind=kOutput, calls=%fused_computation.9 | convolution fusion | flops 2156003328 | bytes 16908288 | tf_op jit(solution)/shard_map/while/body/eval_jaxpr/hxjz,hij->hxiz/dot_general | solution.py:37
  142.4 10.5 %copy.42 = bf16[2,1,64,2,128,128]{5,4,2,0,1,3:T(8,128)(2,1)} copy(bf16[2,1,64,2,128,128]{5,4,3,2,0,1:T(8,128)(2,1)} %bitcast.175) | data formatting | bytes 16777216 | tf_op jit(solution)/shard_map/while/body/eval_jaxpr/reshape | solution.py:50
  153.0 19.5 %all_to_all.34 = bf16[2,1,64,2,128,128]{5,4,2,0,1,3:T(8,128)(2,1)} all-to-all(bf16[2,1,64,2,128,128]{5,4,2,0,1,3:T(8,128)(2,1)} %copy.42), channel_id=1, replica_groups=mesh['grp'=2,'path'=8,'state'=2] {'state'}, dimensions={3} | all-to-all | bytes 16777216 | tf_op jit(solution)/shard_map/while/body/eval_jaxpr/all_to_all | solution.py:51
  172.5 10.5 %copy.43 = bf16[2,2,1,64,1,128,128]{6,5,3,1,0,4,2:T(8,128)(2,1)} copy(bf16[2,2,1,64,1,128,128]{6,5,3,0,1,4,2:T(8,128)(2,1)} %bitcast.177) | data formatting | bytes 16777216 | tf_op jit(solution)/shard_map/while/body/eval_jaxpr/all_to_all | solution.py:51
  183.0 13.3 %reshape.446 = bf16[2,128,16384]{2,1,0:T(8,128)(2,1)} reshape(bf16[2,2,1,64,1,128,128]{6,5,3,1,0,4,2:T(8,128)(2,1)} %copy.43) | data formatting | bytes 16777216 | tf_op jit(solution)/shard_map/while/body/eval_jaxpr/reshape | solution.py:53
  196.3 9.1 %convolution_convert_fusion = bf16[2,128,16384]{2,1,0:T(8,128)(2,1)} fusion(bf16[2,128,128]{2,1,0:T(8,128)(2,1)S(1)} %bitcast.183, bf16[2,128,16384]{2,1,0:T(8,128)(2,1)} %reshape.446), kind=kOutput, calls=%fused_computation.2 | convolution fusion | flops 1077936128 | bytes 16842752 | tf_op jit(solution)/shard_map/while/body/eval_jaxpr/hiw,hwc->hic/dot_general | solution.py:54
  205.4 9.4 %copy.44 = bf16[1,2,16,8,128,128]{5,4,3,1,0,2:T(8,128)(2,1)} copy(bf16[1,2,16,8,128,128]{5,3,4,2,1,0:T(8,128)(2,1)} %bitcast.173) | data formatting | bytes 16777216 | tf_op jit(solution)/shard_map/reshape | solution.py:118
  214.7 7.0 %all-to-all-start.1 = ((bf16[1,2,16,8,128,128]{5,4,3,1,0,2:T(8,128)(2,1)}), bf16[1,2,16,8,128,128]{5,4,3,1,0,2:T(8,128)(2,1)}, u32[]{:S(2)}, u32[]{:S(2)}) async-start(bf16[1,2,16,8,128,128]{5,4,3,1,0,2:T(8,128)(2,1)} %copy.44), calls=%async_computation.1 | async-start | bytes 16777216 | tf_op jit(solution)/shard_map/all_to_all | solution.py:119
  221.8 9.2 %copy.63 = bf16[32,8,128,128]{3,2,1,0:T(8,128)(2,1)} copy(bf16[32,8,128,128]{3,1,2,0:T(8,128)(2,1)} %bitcast.174) | data formatting | bytes 16777216
  231.0 6.1 %fusion.56 = (bf16[1,1,128,128,128]{4,3,2,1,0:T(8,128)(2,1)}, bf16[1,1,128,128,128]{4,3,2,1,0:T(8,128)(2,1)}) fusion(bf16[1,2,128,128,128]{4,3,2,1,0:T(8,128)(2,1)} %bitcast.176), kind=kLoop, calls=%fused_computation.140 | loop fusion | bytes 16777216 | tf_op jit(solution)/shard_map/slice | solution.py:77
  237.1 1.4 gather_fusion
  238.6 1.4 gather_fusion.1
  240.0 174.4 %all_gather.7 = bf16[16,2,8]{2,1,0:T(2,128)(2,1)S(1)} all-gather(bf16[1,2,8]{2,1,0:T(2,128)(2,1)S(1)} %pad_maximum_fusion), channel_id=1, replica_groups=mesh['grp'=2,'path'=8,'state'=2] {'path','state'}, dimensions={0}, use_global_device_ids=true | all-gather | bytes 544 | tf_op jit(solution)/shard_map/all_gather | solution.py:104
  414.6 3.9 fusion.55
  418.5 2.9 multiply_bitcast_fusion
  421.4 4.9 %copy.50 = f32[8,8,2,128,128]{4,3,2,1,0:T(8,128)} copy(f32[8,8,2,128,128]{4,0,3,1,2:T(8,128)S(1)} %multiply_bitcast_fusion) | data formatting | bytes 16777216 | tf_op jit(solution)/shard_map/mul | solution.py:129
  426.3 2.9 multiply_bitcast_fusion.1
  429.1 4.9 %copy.47 = f32[8,8,2,128,128]{4,3,2,1,0:T(8,128)} copy(f32[8,8,2,128,128]{4,0,3,1,2:T(8,128)S(1)} %multiply_bitcast_fusion.1) | data formatting | bytes 16777216 | tf_op jit(solution)/shard_map/mul | solution.py:123
  (39 shorter events, 4.5 us)
Async XLA Ops:
  7.2 126.1 %all-gather.2.cloned.1.call-start = ((), (), s32[]{:S(2)}) async-start(), calls=%async_computation.2 | async-start | bytes 9437184 | tf_op jit(solution)/shard_map/all_gather | solution.py:92
  33.1 11.5 %copy-start = (bf16[3,2,128,128]{3,2,1,0:T(8,128)(2,1)S(1)}, bf16[3,2,128,128]{3,2,1,0:T(8,128)(2,1)}, u32[]{:S(2)}) copy-start(bf16[3,2,128,128]{3,2,1,0:T(8,128)(2,1)} %param.9) | copy-start | bytes 589828
  214.7 7.0 %copy-start.1 = (s32[8]{0:T(128)S(1)}, s32[8]{0:T(128)}, u32[]{:S(2)}) copy-start(s32[8]{0:T(128)} %param.12) | copy-start | bytes 100
  214.7 7.1 %copy-start.2 = (s32[8]{0:T(128)S(1)}, s32[8]{0:T(128)}, u32[]{:S(2)}) copy-start(s32[8]{0:T(128)} %param.13) | copy-start | bytes 100
  214.7 199.8 %all-to-all-start.1 = ((bf16[1,2,16,8,128,128]{5,4,3,1,0,2:T(8,128)(2,1)}), bf16[1,2,16,8,128,128]{5,4,3,1,0,2:T(8,128)(2,1)}, u32[]{:S(2)}, u32[]{:S(2)}) async-start(bf16[1,2,16,8,128,128]{5,4,3,1,0,2:T(8,128)(2,1)} %copy.44), calls=%async_computation.1 | async-start | bytes 16777216 | tf_op jit(solution)/shard_map/all_to_all | solution.py:119
Sparse Core Ops, SparseCore 0:
  10.2 123.0 all-gather.1
where the time goes:
time: 442 us; the launch traced here: 441 us
  blocking collectives  194 us (44%)
  local copies, waits for them, and re-layouts  97.5 us (22%)
  waiting for transfers between devices  88.4 us (20%)
  matrix products  24.9 us (6%)
  between operations  18 us (4%)
  other arithmetic  11.1 us (3%)
  starting transfers between devices  7.03 us (2%)
    all_gather x1, blocking collectives, body(): pooled = lax.all_gather(chosen, ('path', 'state'), axis=0, tiled=True)  174 us
    all_gather x1, waiting for transfers between devices, body(): lax.all_gather(start_states, 'path', axis=2, tiled=True)  87.7 us
    all_to_all x1, blocking collectives, top_block(): lax.all_to_all(shaped, 'state', split_axis=3, concat_axis=1, tiled=True)  19.5 us
    mul x12, local copies, waits for them, and re-layouts, cut_kernel(): result = jnp.kron(result, picked)  19.5 us
    reshape x1, local copies, waits for them, and re-layouts, top_block(): merged = received.reshape(2, dimension, dimension * columns)  13.3 us
    mul x9, other arithmetic, cut_kernel(): result = jnp.kron(result, picked)  10.6 us
    all_to_all x1, local copies, waits for them, and re-layouts, top_block(): lax.all_to_all(shaped, 'state', split_axis=3, concat_axis=1, tiled=True)  10.5 us
    reshape x1, local copies, waits for them, and re-layouts, top_block(): shaped = states.reshape(2, 1, dimension // 2, 2, dimension, dimension)  10.5 us
  transfers between devices with their start and end apart: 2, of which 1 were waited for; matrix products, arithmetic and copies ran while one was open for 12% of the time, Pallas kernels for 0%

commit v1 on v0

v1 whole, which is shorter than its diff:
```python
import functools
import math

import jax
import jax.numpy as jnp
from jax import lax
from jax.experimental import pallas as pl
from jax.experimental.pallas import tpu as pltpu
from jax.sharding import PartitionSpec as P


def mixes(gates, cuts, bits):
    dimension = gates.shape[-1]
    count = bits.shape[1]
    rows = lax.broadcasted_iota(jnp.int32, (dimension, dimension), 0)
    cols = lax.broadcasted_iota(jnp.int32, (dimension, dimension), 1)
    block = 2**count
    kernel = jnp.where(rows // block == cols // block, 1.0, 0.0).astype(jnp.float32)
    for k in reversed(range(count)):
        picked = jnp.where(
            (bits[:, k] == 1)[:, None, None, None], cuts[None, :, k, 1], cuts[None, :, k, 0]
        )
        low_row = rows // 2**k % 2 == 1
        low_col = cols // 2**k % 2 == 1
        entry = [[picked[:, :, a, b, None, None] for b in range(2)] for a in range(2)]
        factor = jnp.where(
            low_row,
            jnp.where(low_col, entry[1][1], entry[1][0]),
            jnp.where(low_col, entry[0][1], entry[0][0]),
        )
        kernel = kernel * factor
    return jnp.einsum(
        "hij,phjk->phik",
        gates.astype(jnp.float32),
        kernel,
        precision=lax.Precision.HIGHEST,
        preferred_element_type=jnp.float32,
    ).astype(jnp.bfloat16)


def turn_kernel(paths, half_block, states_ref, top_ref, middle_ref, out_ref, turned_ref):
    dimension = middle_ref.shape[-1]
    rows = top_ref.shape[0]

    def mix_top(y, carry):
        block = states_ref[:, 0, y].reshape(dimension, dimension)
        turned_ref[pl.ds(y, rows, stride=dimension), :] = jnp.dot(
            top_ref[...], block, preferred_element_type=jnp.float32
        )
        return carry

    lax.fori_loop(0, dimension, mix_top, 0, unroll=4)

    def mix_middle(p, carry):
        matrix = middle_ref[p]
        for side in range(2):
            for w in range(half_block):
                row = (side * paths + p) * half_block + w
                start = pl.multiple_of(row * dimension, dimension)
                block = turned_ref[pl.ds(start, dimension), :].astype(jnp.bfloat16)
                out_ref[side, p, w] = jnp.dot(
                    matrix, block, preferred_element_type=jnp.float32
                ).astype(jnp.bfloat16)
        return carry

    lax.fori_loop(0, paths, mix_middle, 0)


def turn(states, top, middle, u):
    owners, _, dimension, near, _ = states.shape
    paths = middle.shape[0]
    half_block = near // 2
    return pl.pallas_call(
        functools.partial(turn_kernel, paths, half_block),
        grid=(1,),
        in_specs=[
            pl.BlockSpec(
                (owners, 1, dimension, near, dimension),
                lambda i: (0, u, 0, 0, 0),
                pipeline_mode=pl.Buffered(1),
            ),
            pl.BlockSpec(top.shape, lambda i: (0, 0)),
            pl.BlockSpec(middle.shape, lambda i: (0, 0, 0)),
        ],
        out_specs=pl.BlockSpec(
            (2, paths, half_block, dimension, dimension), lambda i: (0, 0, 0, 0, 0)
        ),
        out_shape=jax.ShapeDtypeStruct(
            (2, paths, half_block, dimension, dimension), jnp.bfloat16
        ),
        scratch_shapes=[pltpu.VMEM((top.shape[0] * dimension, dimension), jnp.float32)],
        compiler_params=pltpu.CompilerParams(vmem_limit_bytes=50 * 2**20),
        cost_estimate=pl.CostEstimate(
            flops=4 * top.shape[0] * dimension**3,
            bytes_accessed=4 * dimension**3 * 2,
            transcendentals=0,
        ),
    )(states, top, middle)


def join_kernel(paths, selected, vals_ref, *refs):
    mine = refs[:2]
    other = refs[2:4]
    outs = refs[4:]
    c = vals_ref[2 * paths * selected]
    dimension = mine[0].shape[-1]
    step = 32

    for u in range(2):
        for source, which in ((mine[u], 0), (other[u], 1)):
            half = c if which == 0 else 1.0 - c
            for h in range(2):

                @pl.when(half == float(h))
                def _(source=source, h=h, u=u):
                    def chunk(i, carry):
                        start = pl.multiple_of(i * step, step)
                        loaded = [
                            source[p, 0, pl.ds(start, step), :].astype(jnp.float32)
                            for p in range(paths)
                        ]
                        for j in range(selected):
                            base = (1 - h) * paths * selected + j
                            total = loaded[0] * vals_ref[base]
                            for p in range(1, paths):
                                total = total + loaded[p] * vals_ref[base + p * selected]
                            outs[h][j, 0, u, pl.ds(start, step), :] = total
                        return carry

                    lax.fori_loop(0, dimension // step, chunk, 0)


def join(vals, mine, other):
    paths, half_block, dimension, _ = mine[0].shape
    selected = vals.shape[0] // (2 * paths)
    spec = pl.BlockSpec((paths, 1, dimension, dimension), lambda w, *_: (0, w, 0, 0))
    out_spec = pl.BlockSpec(
        (selected, 1, 2, dimension, dimension), lambda w, *_: (0, w, 0, 0, 0)
    )
    out = jax.ShapeDtypeStruct((selected, half_block, 2, dimension, dimension), jnp.float32)
    return pl.pallas_call(
        functools.partial(join_kernel, paths, selected),
        grid_spec=pltpu.PrefetchScalarGridSpec(
            num_scalar_prefetch=1,
            grid=(half_block,),
            in_specs=[spec] * 4,
            out_specs=[out_spec] * 2,
        ),
        out_shape=[out, out],
        compiler_params=pltpu.CompilerParams(vmem_limit_bytes=50 * 2**20),
    )(vals, *mine, *other)


def body(start_states, block_gates, cut_ops, path_bits, left_pick, right_pick):
    sections = path_bits.shape[1] // 2
    c = lax.axis_index("state")
    k = lax.axis_index("path")
    owners = lax.axis_size("path")
    dimension = start_states.shape[-1]
    half_block = dimension // (2 * owners)
    near = 2 * half_block
    per_device = path_bits.shape[0]
    paths = owners * per_device
    selected = left_pick.shape[0]

    mine = lax.all_to_all(start_states, "state", split_axis=0, concat_axis=1, tiled=True)
    mine = mine.reshape(2, half_block, 2, dimension, dimension)
    laid = jnp.transpose(mine, (2, 3, 0, 1, 4)).reshape(2, dimension, near, dimension)
    gate = lax.dynamic_index_in_dim(block_gates[0], c, 0, keepdims=False)
    base = jnp.einsum(
        "uyvz,iz->uyvi", laid, gate, preferred_element_type=jnp.float32
    ).astype(jnp.bfloat16)

    picks = jnp.stack([left_pick, right_pick])
    own_picks = lax.dynamic_index_in_dim(picks, c, 0, keepdims=False)
    z_hot = (own_picks[:, None] % dimension == jnp.arange(dimension)[None, :]).astype(jnp.bfloat16)
    lanes = jnp.einsum("jz,uyvz->juyv", z_hot, base, preferred_element_type=jnp.float32)
    u_own = own_picks // (dimension * dimension) % 2
    near_pick = jnp.where(u_own[:, None, None] == 1, lanes[:, 1], lanes[:, 0])
    small = jnp.concatenate(
        [
            near_pick.astype(jnp.bfloat16).reshape(-1),
            jnp.pad(path_bits.astype(jnp.bfloat16), ((0, 0), (0, dimension - 2 * sections))).reshape(-1),
        ]
    )
    pooled = lax.all_gather(small, ("path", "state"), axis=0)
    size = selected * dimension * near
    bits = pooled[:, size:].reshape(owners, 2, per_device, dimension)[:, 0, :, : 2 * sections]
    bits = bits.reshape(paths, 2 * sections).astype(jnp.int32)
    columns = pooled[:, :size].reshape(owners, 2, selected, dimension, near)

    gathered = lax.all_gather(base, "path", axis=0)

    mix1 = mixes(block_gates[1], cut_ops[:, :sections], bits[:, :sections])
    mix2 = mixes(block_gates[2], cut_ops[:, sections:], bits[:, sections:])
    turned2 = jnp.transpose(
        mix2.reshape(paths, 2, dimension, 2, owners, half_block), (0, 1, 2, 4, 3, 5)
    ).reshape(paths, 2, dimension, dimension)

    row_y = picks // dimension % dimension
    row_w = picks // (dimension * dimension) // 2
    y_hot = (row_y[:, :, None] == jnp.arange(dimension)).astype(jnp.bfloat16)
    w_hot = (row_w[:, :, None] == jnp.arange(dimension)).astype(jnp.bfloat16)
    m1_rows = jnp.einsum("hjy,phyk->phjk", y_hot, mix1, preferred_element_type=jnp.float32)
    m2_rows = jnp.einsum("hjw,phwv->phjv", w_hot, turned2, preferred_element_type=jnp.float32)
    cols = jnp.transpose(columns, (1, 2, 3, 0, 4)).reshape(2, selected, dimension, dimension)
    first = jnp.einsum(
        "phjy,hjyv->phjv",
        m1_rows.astype(jnp.bfloat16),
        cols,
        preferred_element_type=jnp.float32,
    ).astype(jnp.bfloat16)
    vals = jnp.sum(first.astype(jnp.float32) * m2_rows, axis=-1).astype(jnp.bfloat16)
    scale = 1.0 / math.sqrt(paths)
    flat = jnp.transpose(vals.astype(jnp.float32) * scale, (1, 0, 2)).reshape(-1)
    flat = jnp.concatenate([flat, c.astype(jnp.float32)[None]])

    own2 = lax.dynamic_index_in_dim(turned2, c, 1, keepdims=False)
    own2 = own2.reshape(paths, 2, owners, half_block, dimension)
    own2 = lax.dynamic_index_in_dim(own2, k, 2, keepdims=False)
    own2 = jnp.where(c == 1, own2[:, ::-1], own2)
    top = jnp.transpose(own2, (1, 0, 2, 3)).reshape(2 * paths * half_block, dimension)
    middle = lax.dynamic_index_in_dim(mix1, c, 1, keepdims=False)

    kept, arrived = [], []
    for u in range(2):
        both = turn(gathered, top, middle, u)
        kept.append(both[0])
        arrived.append(lax.ppermute(both[1], "state", [(0, 1), (1, 0)]))
    outs = join(flat, kept, arrived)
    return tuple(out.reshape(selected, 1, near, dimension, dimension) for out in outs)


def solution(mesh):
    in_specs = (P(None, "state", "path", None, None), P(), P(), P(("grp", "path"), None), P(), P())
    out_specs = (P("grp", "state", "path", None, None), P("grp", "state", "path", None, None))
    return jax.shard_map(body, mesh=mesh, in_specs=in_specs, out_specs=out_specs, check_vma=False)
```

time: 442 us -> 221 us (0.50)
  blocking collectives: 194 us -> 26.9 us
  local copies, waits for them, and re-layouts: 97.5 us -> 21.7 us
  Pallas kernels: 0 us -> 48.5 us
  matrix products: 24.9 us -> 5.31 us
  other arithmetic: 11.1 us -> 1.07 us
  waiting for transfers between devices: 88.4 us -> 92.9 us
    all_gather x1, blocking collectives: 174 us -> 26.9 us  [body(): pooled = lax.all_gather(small, ('path', 'state'), axis=0)]
    pallas_call x0 -> x3, Pallas kernels: none -> 48.5 us  [the longest x2 33.3 us: turn(): pl.pallas_call(functools.partial(turn_kernel, paths, half_block), grid=(1...]
    mul x14 -> x1, local copies, waits for them, and re-layouts: 29.3 us -> 0.07 us  [body(): vals.astype(jnp.float32) * scale]
    reshape x3 -> x5, local copies, waits for them, and re-layouts: 33.1 us -> 5.04 us  [the longest x1 4.73 us: body(): columns = pooled[:, :size].reshape(owners, 2, selected, dimension, near)]
    dot_general x8 -> x7, matrix products: 24.9 us -> 5.31 us  [the longest x2 2.56 us: mixes(): jnp.einsum('hij,phjk->phik', gates.astype(jnp.float32), kernel, precision...]
    all_to_all x1 -> x0, blocking collectives: 19.5 us -> none  [top_block(): lax.all_to_all(shaped, 'state', split_axis=3, concat_axis=1, tiled=True)]
    slice x4 -> x8, local copies, waits for them, and re-layouts: 11.6 us -> 0.53 us  [the longest x3 0.39 us: body(): near_pick = jnp.where(u_own[:, None, None] == 1, lanes[:, 1], lanes[:, 0])]
    mul x9 -> x1, other arithmetic: 10.6 us -> 0.01 us  [body(): vals.astype(jnp.float32) * scale]
  transfers between devices with their start and end apart: 2 -> 4, of which waited for: 1 -> 2; matrix products, arithmetic and copies ran while one was open for 12% -> 8% of each run, Pallas kernels for 0% -> 0%
where the time goes in v1:
time: 221 us; the launch traced here: 217 us
  waiting for transfers between devices  92.9 us (42%)
  Pallas kernels  48.5 us (22%)
  blocking collectives  26.9 us (12%)
  local copies, waits for them, and re-layouts  21.7 us (10%)
  between operations  14.5 us (7%)
  starting transfers between devices  5.79 us (3%)
  matrix products  5.31 us (2%)
    all_gather x1, waiting for transfers between devices, body(): gathered = lax.all_gather(base, 'path', axis=0)  91.1 us
    pallas_call x2, Pallas kernels, turn(): pl.pallas_call(functools.partial(turn_kernel, paths, half_block), grid=(1...  33.3 us
    all_gather x1, blocking collectives, body(): pooled = lax.all_gather(small, ('path', 'state'), axis=0)  26.9 us
    pallas_call x1, Pallas kernels, join(): pl.pallas_call(functools.partial(join_kernel, paths, selected), grid_spec...  15.2 us
    squeeze x2, local copies, waits for them, and re-layouts, body(): arrived.append(lax.ppermute(both[1], 'state', [(0, 1), (1, 0)]))  6.68 us
    reshape x1, local copies, waits for them, and re-layouts, body(): columns = pooled[:, :size].reshape(owners, 2, selected, dimension, near)  4.73 us
  transfers between devices with their start and end apart: 4, of which 2 were waited for; matrix products, arithmetic and copies ran while one was open for 8% of the time, Pallas kernels for 0%

profile of v1, /device:TPU:9, one launch (start us, length us, event | category | flops | bytes accessed | tf_op | source)
XLA Modules:
  0.0 216.5 jit_solution(3703513753035005351)
XLA Ops:
  7.2 4.4 %all-to-all-start = ((bf16[2,1,16,128,128]{4,3,2,1,0:T(8,128)(2,1)}), bf16[2,1,16,128,128]{4,3,2,1,0:T(8,128)(2,1)S(1)}, u32[]{:S(2)}, u32[]{:S(2)}) async-start(bf16[2,1,16,128,128]{4,3,2,1,0:T(8,128)(2,1)} %param.6), calls=%async_computation | async-start | bytes 2097152 | tf_op jit(solution)/shard_map/all_to_all | solution.py:166
  11.6 1.7 all-to-all-done
  13.4 0.4 fusion
  13.9 1.7 copy.106
  17.3 0.2 broadcast_in_dim.392
  17.5 0.3 fusion.103
  17.8 0.2 copy.85
  18.0 0.2 squeeze.51
  18.2 0.2 copy.84
  18.4 0.2 squeeze.50
  18.7 26.9 %all-gather.2 = bf16[16,1,16512]{2,1,0:T(2,128)(2,1)S(1)} all-gather(bf16[1,1,16512]{2,1,0:T(2,128)(2,1)S(1)} %reshape.414), channel_id=2, replica_groups=mesh['grp'=2,'path'=8,'state'=2] {'path','state'}, dimensions={0}, use_global_device_ids=true | all-gather | bytes 561408 | tf_op jit(solution)/shard_map/all_gather | solution.py:186
  45.7 0.3 fusion.105
  46.2 0.1 fusion.73
  46.4 0.1 fusion.71
  46.5 0.1 fusion.89
  46.6 1.3 convolution_convert_fusion.1
  48.0 0.8 copy-done.1
  48.9 0.2 copy.107
  49.3 1.3 convolution_convert_fusion.2
  50.6 0.8 copy-done.3
  51.4 91.1 %all-gather.5.cloned.1.call-done = bf16[16,128,16,128]{3,2,1,0:T(8,128)(2,1)} async-done(((bf16[2,128,16,128]{3,2,1,0:T(8,128)(2,1)}), bf16[16,128,16,128]{3,2,1,0:T(8,128)(2,1)}) %all-gather.5.cloned.1.call-update) | async-done | bytes 8388624 | tf_op jit(solution)/shard_map/all_gather | solution.py:192
  142.5 16.7 %shard_map.78 = bf16[2,8,8,128,128]{4,3,2,1,0:T(8,128)(2,1)} custom-call(bf16[8,2,128,16,128]{4,3,2,1,0:T(8,128)(2,1)} %bitcast.177, bf16[128,128]{1,0:T(8,128)(2,1)S(1)} %bitcast.175, bf16[8,128,128]{2,1,0:T(8,128)(2,1)S(1)} %dynamic-slice_bitcast_fusion.middle_ref), custom_call_target="tpu_custom_call" | custom-call | flops 1073741824 | bytes 16777216 | tf_op jit(solution)/shard_map/pallas_call | solution.py:73
  159.2 16.7 %shard_map.77 = bf16[2,8,8,128,128]{4,3,2,1,0:T(8,128)(2,1)} custom-call(bf16[8,2,128,16,128]{4,3,2,1,0:T(8,128)(2,1)} %bitcast.178, bf16[128,128]{1,0:T(8,128)(2,1)S(1)} %bitcast.176, bf16[8,128,128]{2,1,0:T(8,128)(2,1)S(1)} %dynamic-slice_bitcast_fusion.middle_ref), custom_call_target="tpu_custom_call" | custom-call | flops 1073741824 | bytes 16777216 | tf_op jit(solution)/shard_map/pallas_call | solution.py:73
  175.8 4.2 %slice_bitcast_fusion.1 = (bf16[8,8,128,128]{3,2,1,0:T(8,128)(2,1)}, bf16[8,8,128,128]{3,2,1,0:T(8,128)(2,1)S(1)}) fusion(bf16[2,8,8,128,128]{4,3,2,1,0:T(8,128)(2,1)} %shard_map.77), kind=kLoop, calls=%fused_computation.1 | loop fusion | bytes 8388608 | tf_op jit(solution)/shard_map/squeeze | solution.py:229
  180.0 2.5 %slice_bitcast_fusion = (bf16[8,8,128,128]{3,2,1,0:T(8,128)(2,1)}, bf16[8,8,128,128]{3,2,1,0:T(8,128)(2,1)}) fusion(bf16[2,8,8,128,128]{4,3,2,1,0:T(8,128)(2,1)S(1)} %copy-done), kind=kLoop, calls=%fused_computation | loop fusion | bytes 8388608 | tf_op jit(solution)/shard_map/squeeze | solution.py:229
  182.5 1.4 collective-permute-start.1
  184.0 4.7 %reshape.401 = bf16[8,2,8,128,16]{4,3,2,1,0:T(8,128)(2,1)} reshape(bf16[16,16384]{1,0:T(8,128)(2,1)S(1)} %slice.240) | data formatting | bytes 1048576 | tf_op jit(solution)/shard_map/reshape | solution.py:190
  188.7 3.6 %copy.86 = bf16[2,8,128,8,16]{2,4,3,1,0:T(8,128)(2,1)S(1)} copy(bf16[2,8,128,8,16]{4,2,1,0,3:T(8,128)(2,1)} %bitcast.179) | data formatting | bytes 1048576 | tf_op jit(solution)/shard_map/transpose | solution.py:206
  192.3 1.3 fusion.5
  193.5 0.3 fusion.30
  193.8 0.5 fusion.4
  194.5 15.2 %shard_map.79 = (f32[8,8,2,128,128]{4,3,2,1,0:T(8,128)}, f32[8,8,2,128,128]{4,3,2,1,0:T(8,128)}) custom-call(f32[129]{0:T(256)S(1)} %pad_maximum_fusion.1.vals_ref, bf16[8,8,128,128]{3,2,1,0:T(8,128)(2,1)S(1)} %get-tuple-element.23.refs_0_, bf16[8,8,128,128]{3,2,1,0:T(8,128)(2,1)} %get-tuple-element.21.refs_1_, ...), custom_call_target="tpu_custom_call" | custom-call | tf_op jit(solution)/shard_map/pallas_call | solution.py:141
  (76 shorter events, 2.6 us)
Async XLA Ops:
  7.2 6.3 %slice-start = ((bf16[3,2,128,128]{3,2,1,0:T(8,128)(2,1)}), bf16[1,2,128,128]{3,2,1,0:T(8,128)(2,1)S(1)}, s32[]{:S(2)}) async-start(bf16[3,2,128,128]{3,2,1,0:T(8,128)(2,1)} %param.7), calls=%async_computation.2 | async-start | bytes 131072 | tf_op jit(solution)/shard_map/slice | solution.py:169
  7.2 6.1 %all-to-all-start = ((bf16[2,1,16,128,128]{4,3,2,1,0:T(8,128)(2,1)}), bf16[2,1,16,128,128]{4,3,2,1,0:T(8,128)(2,1)S(1)}, u32[]{:S(2)}, u32[]{:S(2)}) async-start(bf16[2,1,16,128,128]{4,3,2,1,0:T(8,128)(2,1)} %param.6), calls=%async_computation | async-start | bytes 2097152 | tf_op jit(solution)/shard_map/all_to_all | solution.py:166
  11.6 131.0 %all-gather.5.cloned.1.call-start = ((), (), s32[]{:S(2)}) async-start(), calls=%async_computation.1 | async-start | bytes 9437184 | tf_op jit(solution)/shard_map/all_gather | solution.py:192
  13.9 1.8 copy-start.8
  13.9 1.8 copy-start.4
  13.9 3.2 %copy-start.6 = (s32[8]{0:T(128)S(1)}, s32[8]{0:T(128)}, u32[]{:S(2)}) copy-start(s32[8]{0:T(128)} %param.11) | copy-start | bytes 100
  13.9 3.2 %copy-start.7 = (s32[8]{0:T(128)S(1)}, s32[8]{0:T(128)}, u32[]{:S(2)}) copy-start(s32[8]{0:T(128)} %param.10) | copy-start | bytes 100
  18.0 28.6 %copy-start.5 = (bf16[3,2,128,128]{3,2,1,0:T(8,128)(2,1)S(1)}, bf16[3,2,128,128]{3,2,1,0:T(8,128)(2,1)}, u32[]{:S(2)}) copy-start(bf16[3,2,128,128]{3,2,1,0:T(8,128)(2,1)} %param.7) | copy-start | bytes 589828
  48.0 0.9 copy-start.1
  50.6 0.8 copy-start.3
  175.8 4.2 %copy-start = (bf16[2,8,8,128,128]{4,3,2,1,0:T(8,128)(2,1)S(1)}, bf16[2,8,8,128,128]{4,3,2,1,0:T(8,128)(2,1)}, u32[]{:S(2)}) copy-start(bf16[2,8,8,128,128]{4,3,2,1,0:T(8,128)(2,1)} %shard_map.78) | copy-start | bytes 12582916
  182.5 12.0 %collective-permute-start.1 = (bf16[8,8,128,128]{3,2,1,0:T(8,128)(2,1)}, bf16[8,8,128,128]{3,2,1,0:T(8,128)(2,1)}, u32[]{:S(2)}, u32[]{:S(2)}) collective-permute-start(bf16[8,8,128,128]{3,2,1,0:T(8,128)(2,1)} %get-tuple-element.20), channel_id=1, source_target_pairs={{0,1},{1,0},{2,3},{3,2},{4,5},{5,4},{6,7},{7,6},{8,9},{9,8},{10,11... | collective-permute-start | bytes 6291464 | tf_op jit(solution)/shard_map/ppermute | solution.py:229
  183.9 10.6 %collective-permute-start = (bf16[8,8,128,128]{3,2,1,0:T(8,128)(2,1)}, bf16[8,8,128,128]{3,2,1,0:T(8,128)(2,1)}, u32[]{:S(2)}, u32[]{:S(2)}) collective-permute-start(bf16[8,8,128,128]{3,2,1,0:T(8,128)(2,1)} %get-tuple-element.22), channel_id=1, source_target_pairs={{0,1},{1,0},{2,3},{3,2},{4,5},{5,4},{6,7},{7,6},{8,9},{9,8},{10,11... | collective-permute-start | bytes 6291464 | tf_op jit(solution)/shard_map/ppermute | solution.py:229
  188.7 4.8 %copy-start.2 = (bf16[8,2,128,2,8,8]{2,5,3,4,1,0:T(8,128)(2,1)S(1)}, bf16[8,2,128,2,8,8]{2,5,3,4,1,0:T(8,128)(2,1)}, u32[]{:S(2)}) copy-start(bf16[8,2,128,2,8,8]{2,5,3,4,1,0:T(8,128)(2,1)} %copy-done.1) | copy-start | bytes 1572868
Sparse Core Ops, SparseCore 0:
  15.7 126.7 all-gather.4

commit v2 on v1

--- a/solution.py
+++ b/solution.py
@@ -7,6 +7,138 @@
 from jax.experimental import pallas as pl
 from jax.experimental.pallas import tpu as pltpu
 from jax.sharding import PartitionSpec as P
+
+
+MESH = pl.DeviceIdType.MESH
+
+
+def gather_kernel(n, pairs, base_ref, out_ref, own_sem, send_sem, recv_sem):
+    g, k, c = lax.axis_index("grp"), lax.axis_index("path"), lax.axis_index("state")
+    dimension = base_ref.shape[1]
+    odd = lax.rem(k, 2)
+    pos = (1 - odd) * (k // 2) + odd * (n - 1 - k // 2)
+
+    def place(p):
+        p = lax.rem(p + n, n)
+        high = p // (n // 2)
+        return (1 - high) * (2 * p) + high * (2 * (n - 1 - p) + 1)
+
+    right, left = (g, place(pos + 1), c), (g, place(pos - 1), c)
+    side = lax.rem(g, 2) if pairs else 0
+    partner = (g + 1 - 2 * side, k, c)
+
+    barrier = pltpu.get_barrier_semaphore()
+    greeted = (right, left, partner) if pairs else (right, left)
+    for other in greeted:
+        pl.semaphore_signal(barrier, inc=1, device_id=other, device_id_type=MESH)
+    pl.semaphore_wait(barrier, len(greeted))
+
+    outer = (dimension + 2) // 3 if pairs else dimension // 2
+    middle = dimension - 2 * outer if pairs else dimension - outer
+
+    def cut(start, length):
+        first = (length + 1) // 2
+        return ((start, first), (start + first, length - first))
+
+    far = dimension - outer
+    runs = (
+        cut(side * far if pairs else 0, outer),
+        cut(outer, middle),
+        cut((1 - side) * far if pairs else 0, outer),
+    )
+
+    own = pltpu.make_async_copy(base_ref, out_ref.at[k], own_sem)
+    own.start()
+
+    def copy(stream, u, step, piece, target):
+        start, length = runs[stream][piece]
+        hop = (step - 1, 1 - step, step)[stream]
+        rows = pl.ds(start, length)
+        block = place(pos - hop)
+        source = base_ref.at[u, rows] if stream < 2 and step == 1 else out_ref.at[block, u, rows]
+        return pltpu.make_async_remote_copy(
+            src_ref=source,
+            dst_ref=out_ref.at[block, u, rows],
+            send_sem=send_sem.at[stream, u, step - 1, piece],
+            recv_sem=recv_sem.at[stream, u, step - 1, piece],
+            device_id=target,
+            device_id_type=MESH,
+        )
+
+    def arriving(stream, u, step, piece):
+        start, length = runs[stream][piece]
+        hop = (step, -step, step)[stream]
+        ref = out_ref.at[place(pos - hop), u, pl.ds(start, length)]
+        return pltpu.make_async_remote_copy(
+            src_ref=ref,
+            dst_ref=ref,
+            send_sem=send_sem.at[stream, u, step - 1, piece],
+            recv_sem=recv_sem.at[stream, u, step - 1, piece],
+            device_id=left,
+            device_id_type=MESH,
+        )
+
+    started = []
+
+    def start(item):
+        item.start()
+        started.append(item)
+
+    def advance(u, step):
+        for piece in range(2):
+            for stream, target in ((0, right), (1, left)):
+                if step > 0:
+                    arriving(stream, u, step, piece).wait_recv()
+                if step < n - 1:
+                    start(copy(stream, u, step + 1, piece, target))
+                if pairs and stream == 0 and step > 0:
+                    start(passed(u, step, piece))
+
+    def passed(u, step, piece):
+        first, length = runs[0][piece]
+        ref = out_ref.at[place(pos - step), u, pl.ds(first, length)]
+        return pltpu.make_async_remote_copy(
+            src_ref=ref,
+            dst_ref=ref,
+            send_sem=send_sem.at[2, u, step - 1, piece],
+            recv_sem=recv_sem.at[2, u, step - 1, piece],
+            device_id=partner,
+            device_id_type=MESH,
+        )
+
+    for step in range(n - 1):
+        advance(0, step)
+    advance(1, 0)
+    advance(0, n - 1)
+    for step in range(1, n):
+        advance(1, step)
+    if pairs:
+        for u in range(2):
+            for step in range(1, n):
+                for piece in range(2):
+                    arriving(2, u, step, piece).wait_recv()
+    for item in started:
+        item.wait_send()
+    own.wait()
+
+
+def gather_rows(base, n):
+    pairs = lax.axis_size("grp") % 2 == 0
+    streams = 3 if pairs else 2
+    return pl.pallas_call(
+        functools.partial(gather_kernel, n, pairs),
+        out_shape=jax.ShapeDtypeStruct((n,) + base.shape, base.dtype),
+        in_specs=[pl.BlockSpec(memory_space=pltpu.VMEM)],
+        out_specs=pl.BlockSpec(memory_space=pl.ANY),
+        scratch_shapes=[
+            pltpu.SemaphoreType.DMA,
+            pltpu.SemaphoreType.DMA((streams, 2, n - 1, 2)),
+            pltpu.SemaphoreType.DMA((streams, 2, n - 1, 2)),
+        ],
+        compiler_params=pltpu.CompilerParams(
+            collective_id=0, has_side_effects=True, vmem_limit_bytes=8 * 2**20
+        ),
+    )(base)
 
 
 def mixes(gates, cuts, bits):
@@ -189,7 +321,11 @@
     bits = bits.reshape(paths, 2 * sections).astype(jnp.int32)
     columns = pooled[:, :size].reshape(owners, 2, selected, dimension, near)
 
-    gathered = lax.all_gather(base, "path", axis=0)
+    if owners % 2 == 0 and 4 <= owners <= 8:
+        base, bits = lax.optimization_barrier((base, bits))
+        gathered = gather_rows(base, owners)
+    else:
+        gathered = lax.all_gather(base, "path", axis=0)
 
     mix1 = mixes(block_gates[1], cut_ops[:, :sections], bits[:, :sections])
     mix2 = mixes(block_gates[2], cut_ops[:, sections:], bits[:, sections:])

time: 221 us -> 176 us (0.80)
  waiting for transfers between devices: 92.9 us -> 0.1 us
  Pallas kernels: 48.5 us -> 110 us
  between operations: 14.5 us -> 1.12 us
  blocking collectives: 26.9 us -> 22.2 us
  starting transfers between devices: 5.79 us -> 9.68 us
    all_gather x1 -> x0, waiting for transfers between devices: 91.1 us -> none  [body(): gathered = lax.all_gather(base, 'path', axis=0)]
    pallas_call x0 -> x1, Pallas kernels: none -> 61.6 us  [gather_rows(): pl.pallas_call(functools.partial(gather_kernel, n, pairs), out_shape=jax....]
    all_gather x1, blocking collectives: 26.9 us -> 22.2 us  [body(): pooled = lax.all_gather(small, ('path', 'state'), axis=0)]
    ppermute x2, starting transfers between devices: 1.4 us -> 5.29 us  [body(): arrived.append(lax.ppermute(both[1], 'state', [(0, 1), (1, 0)]))]
  transfers between devices with their start and end apart: 4 -> 3, of which waited for: 2 -> 1; matrix products, arithmetic and copies ran while one was open for 8% -> 9% of each run, Pallas kernels for 0% -> 10%
where the time goes in v2:
time: 176 us; the launch traced here: 174 us
  Pallas kernels  110 us (62%)
  local copies, waits for them, and re-layouts  23.8 us (14%)
  blocking collectives  22.2 us (13%)
  starting transfers between devices  9.68 us (6%)
  matrix products  5.72 us (3%)
    pallas_call x1, Pallas kernels, gather_rows(): pl.pallas_call(functools.partial(gather_kernel, n, pairs), out_shape=jax....  61.6 us
    pallas_call x2, Pallas kernels, turn(): pl.pallas_call(functools.partial(turn_kernel, paths, half_block), grid=(1...  33.3 us
    all_gather x1, blocking collectives, body(): pooled = lax.all_gather(small, ('path', 'state'), axis=0)  22.2 us
    pallas_call x1, Pallas kernels, join(): pl.pallas_call(functools.partial(join_kernel, paths, selected), grid_spec...  15.2 us
    squeeze x2, local copies, waits for them, and re-layouts, body(): arrived.append(lax.ppermute(both[1], 'state', [(0, 1), (1, 0)]))  8.83 us
    ppermute x2, starting transfers between devices, body(): arrived.append(lax.ppermute(both[1], 'state', [(0, 1), (1, 0)]))  5.29 us
    reshape x1, local copies, waits for them, and re-layouts, body(): columns = pooled[:, :size].reshape(owners, 2, selected, dimension, near)  4.73 us
    all_to_all x1, starting transfers between devices, body(): lax.all_to_all(start_states, 'state', split_axis=0, concat_axis=1, tiled=...  4.39 us
  transfers between devices with their start and end apart: 3, of which 1 were waited for; matrix products, arithmetic and copies ran while one was open for 9% of the time, Pallas kernels for 10%

profile of v2, /device:TPU:9, one launch (start us, length us, event | category | flops | bytes accessed | tf_op | source)
XLA Modules:
  0.0 173.7 jit_solution(10491241727770420634)
XLA Ops:
  0.7 4.4 %all-to-all-start = ((bf16[2,1,16,128,128]{4,3,2,1,0:T(8,128)(2,1)}), bf16[2,1,16,128,128]{4,3,2,1,0:T(8,128)(2,1)S(1)}, u32[]{:S(2)}, u32[]{:S(2)}) async-start(bf16[2,1,16,128,128]{4,3,2,1,0:T(8,128)(2,1)} %param.6), calls=%async_computation | async-start | bytes 2097152 | tf_op jit(solution)/shard_map/all_to_all | solution.py:298
  5.4 0.1 copy.123
  5.5 0.1 copy.132
  6.8 0.7 fusion.base_ref
  7.6 0.4 fusion.7
  8.0 0.1 broadcast_in_dim.391
  8.1 0.2 broadcast_in_dim.392
  8.3 0.2 copy.86
  8.5 0.2 squeeze.51
  8.7 0.2 copy.85
  8.9 0.2 squeeze.50
  9.2 22.2 %all-gather.1 = bf16[16,1,16512]{2,1,0:T(2,128)(2,1)S(1)} all-gather(bf16[1,1,16512]{2,1,0:T(2,128)(2,1)S(1)} %reshape.413), channel_id=2, replica_groups=mesh['grp'=2,'path'=8,'state'=2] {'path','state'}, dimensions={0}, use_global_device_ids=true | all-gather | bytes 561408 | tf_op jit(solution)/shard_map/all_gather | solution.py:318
  31.5 0.3 fusion.107
  32.1 0.1 fusion.76
  32.2 0.1 fusion.74
  32.4 0.1 fusion.92
  32.5 1.3 convolution_convert_fusion.2
  33.8 1.3 convolution_convert_fusion.1
  35.3 0.2 copy.107
  35.5 61.6 %shard_map.77.states_ref = bf16[8,2,128,16,128]{4,3,2,1,0:T(8,128)(2,1)S(1)} custom-call(bf16[2,128,16,128]{3,2,1,0:T(8,128)(2,1)S(1)} %fusion.base_ref), custom_call_target="tpu_custom_call" | custom-call | tf_op jit(solution)/shard_map/pallas_call | solution.py:128
  97.1 3.4 %copy-done = bf16[8,2,128,16,128]{4,3,2,1,0:T(8,128)(2,1)} copy-done((bf16[8,2,128,16,128]{4,3,2,1,0:T(8,128)(2,1)}, bf16[8,2,128,16,128]{4,3,2,1,0:T(8,128)(2,1)S(1)}, u32[]{:S(2)}) %copy-start) | copy-done | bytes 8388632
  100.5 16.6 %shard_map.79 = bf16[2,8,8,128,128]{4,3,2,1,0:T(8,128)(2,1)} custom-call(bf16[8,2,128,16,128]{4,3,2,1,0:T(8,128)(2,1)} %copy-done, bf16[128,128]{1,0:T(8,128)(2,1)S(1)} %bitcast.173, bf16[8,128,128]{2,1,0:T(8,128)(2,1)S(1)} %dynamic-slice_bitcast_fusion.middle_ref), custom_call_target="tpu_custom_call" | custom-call | flops 1073741824 | bytes 16777216 | tf_op jit(solution)/shard_map/pallas_call | solution.py:205
  117.1 4.8 %slice_bitcast_fusion = (bf16[8,8,128,128]{3,2,1,0:T(8,128)(2,1)}, bf16[8,8,128,128]{3,2,1,0:T(8,128)(2,1)}) fusion(bf16[2,8,8,128,128]{4,3,2,1,0:T(8,128)(2,1)} %shard_map.79), kind=kLoop, calls=%fused_computation | loop fusion | bytes 8388608 | tf_op jit(solution)/shard_map/squeeze | solution.py:365
  121.9 5.3 %collective-permute-start.1 = (bf16[8,8,128,128]{3,2,1,0:T(8,128)(2,1)}, bf16[8,8,128,128]{3,2,1,0:T(8,128)(2,1)}, u32[]{:S(2)}, u32[]{:S(2)}) collective-permute-start(bf16[8,8,128,128]{3,2,1,0:T(8,128)(2,1)} %get-tuple-element.24), channel_id=1, source_target_pairs={{0,1},{1,0},{2,3},{3,2},{4,5},{5,4},{6,7},{7,6},{8,9},{9,8},{10,11... | collective-permute-start | bytes 6291464 | tf_op jit(solution)/shard_map/ppermute | solution.py:365
  127.2 16.6 %shard_map.78 = bf16[2,8,8,128,128]{4,3,2,1,0:T(8,128)(2,1)} custom-call(bf16[8,2,128,16,128]{4,3,2,1,0:T(8,128)(2,1)} %copy-done, bf16[128,128]{1,0:T(8,128)(2,1)S(1)} %bitcast.174, bf16[8,128,128]{2,1,0:T(8,128)(2,1)S(1)} %dynamic-slice_bitcast_fusion.middle_ref), custom_call_target="tpu_custom_call" | custom-call | flops 1073741824 | bytes 16777216 | tf_op jit(solution)/shard_map/pallas_call | solution.py:205
  143.8 4.1 %slice_bitcast_fusion.1 = (bf16[8,8,128,128]{3,2,1,0:T(8,128)(2,1)}, bf16[8,8,128,128]{3,2,1,0:T(8,128)(2,1)S(1)}) fusion(bf16[2,8,8,128,128]{4,3,2,1,0:T(8,128)(2,1)} %shard_map.78), kind=kLoop, calls=%fused_computation.1 | loop fusion | bytes 8388608 | tf_op jit(solution)/shard_map/squeeze | solution.py:365
  147.9 4.7 %reshape.401 = bf16[8,2,8,128,16]{4,3,2,1,0:T(8,128)(2,1)} reshape(bf16[16,16384]{1,0:T(8,128)(2,1)S(1)} %slice.240) | data formatting | bytes 1048576 | tf_op jit(solution)/shard_map/reshape | solution.py:322
  152.7 3.6 %copy.87 = bf16[2,8,128,8,16]{2,4,3,1,0:T(8,128)(2,1)S(1)} copy(bf16[2,8,128,8,16]{4,2,1,0,3:T(8,128)(2,1)} %bitcast.175) | data formatting | bytes 1048576 | tf_op jit(solution)/shard_map/transpose | solution.py:342
  156.2 0.2 fusion.5
  156.5 1.3 fusion.33
  157.8 0.5 fusion.4
  158.5 15.2 %shard_map.80 = (f32[8,8,2,128,128]{4,3,2,1,0:T(8,128)}, f32[8,8,2,128,128]{4,3,2,1,0:T(8,128)}) custom-call(f32[129]{0:T(256)S(1)} %pad_maximum_fusion.1.vals_ref, bf16[8,8,128,128]{3,2,1,0:T(8,128)(2,1)S(1)} %get-tuple-element.27.refs_0_, bf16[8,8,128,128]{3,2,1,0:T(8,128)(2,1)} %get-tuple-element.25.refs_1_, ...), custom_call_target="tpu_custom_call" | custom-call | tf_op jit(solution)/shard_map/pallas_call | solution.py:273
  (72 shorter events, 2.3 us)
Async XLA Ops:
  0.6 4.5 %copy-start.6 = (s32[8]{0:T(128)S(1)}, s32[8]{0:T(128)}, u32[]{:S(2)}) copy-start(s32[8]{0:T(128)} %param.11) | copy-start | bytes 100
  0.6 4.5 %copy-start.7 = (s32[8]{0:T(128)S(1)}, s32[8]{0:T(128)}, u32[]{:S(2)}) copy-start(s32[8]{0:T(128)} %param.10) | copy-start | bytes 100
  0.7 4.6 %copy-start.8 = (s32[1,6]{1,0:T(1,128)S(1)}, s32[1,6]{1,0:T(1,128)}, u32[]{:S(2)}) copy-start(s32[1,6]{1,0:T(1,128)} %param.9) | copy-start | bytes 76
  0.7 4.6 %copy-start.4 = (f32[2,6,2,2,2]{1,4,3,2,0:T(2,128)S(1)}, f32[2,6,2,2,2]{1,4,3,2,0:T(2,128)}, u32[]{:S(2)}) copy-start(f32[2,6,2,2,2]{1,4,3,2,0:T(2,128)} %param.8) | copy-start | bytes 1156
  0.7 6.2 %slice-start = ((bf16[3,2,128,128]{3,2,1,0:T(8,128)(2,1)}), bf16[1,2,128,128]{3,2,1,0:T(8,128)(2,1)S(1)}, s32[]{:S(2)}) async-start(bf16[3,2,128,128]{3,2,1,0:T(8,128)(2,1)} %param.7), calls=%async_computation.1 | async-start | bytes 131072 | tf_op jit(solution)/shard_map/slice | solution.py:301
  0.7 6.1 %all-to-all-start = ((bf16[2,1,16,128,128]{4,3,2,1,0:T(8,128)(2,1)}), bf16[2,1,16,128,128]{4,3,2,1,0:T(8,128)(2,1)S(1)}, u32[]{:S(2)}, u32[]{:S(2)}) async-start(bf16[2,1,16,128,128]{4,3,2,1,0:T(8,128)(2,1)} %param.6), calls=%async_computation | async-start | bytes 2097152 | tf_op jit(solution)/shard_map/all_to_all | solution.py:298
  8.5 23.9 %copy-start.5 = (bf16[3,2,128,128]{3,2,1,0:T(8,128)(2,1)S(1)}, bf16[3,2,128,128]{3,2,1,0:T(8,128)(2,1)}, u32[]{:S(2)}) copy-start(bf16[3,2,128,128]{3,2,1,0:T(8,128)(2,1)} %param.7) | copy-start | bytes 589828
  33.8 1.3 copy-start.1
  35.2 81.9 %copy-start.3 = (bf16[8,2,128,2,8,8]{2,5,3,4,1,0:T(8,128)(2,1)}, bf16[8,2,128,2,8,8]{2,5,3,4,1,0:T(8,128)(2,1)S(1)}, u32[]{:S(2)}) copy-start(bf16[8,2,128,2,8,8]{2,5,3,4,1,0:T(8,128)(2,1)S(1)} %copy.103) | copy-start | bytes 1572868
  97.1 3.4 %copy-start = (bf16[8,2,128,16,128]{4,3,2,1,0:T(8,128)(2,1)}, bf16[8,2,128,16,128]{4,3,2,1,0:T(8,128)(2,1)S(1)}, u32[]{:S(2)}) copy-start(bf16[8,2,128,16,128]{4,3,2,1,0:T(8,128)(2,1)S(1)} %shard_map.77.states_ref) | copy-start | bytes 25165828
  121.9 36.6 %collective-permute-start.1 = (bf16[8,8,128,128]{3,2,1,0:T(8,128)(2,1)}, bf16[8,8,128,128]{3,2,1,0:T(8,128)(2,1)}, u32[]{:S(2)}, u32[]{:S(2)}) collective-permute-start(bf16[8,8,128,128]{3,2,1,0:T(8,128)(2,1)} %get-tuple-element.24), channel_id=1, source_target_pairs={{0,1},{1,0},{2,3},{3,2},{4,5},{5,4},{6,7},{7,6},{8,9},{9,8},{10,11... | collective-permute-start | bytes 6291464 | tf_op jit(solution)/shard_map/ppermute | solution.py:365
  147.9 10.6 %collective-permute-start = (bf16[8,8,128,128]{3,2,1,0:T(8,128)(2,1)}, bf16[8,8,128,128]{3,2,1,0:T(8,128)(2,1)}, u32[]{:S(2)}, u32[]{:S(2)}) collective-permute-start(bf16[8,8,128,128]{3,2,1,0:T(8,128)(2,1)} %get-tuple-element.26), channel_id=1, source_target_pairs={{0,1},{1,0},{2,3},{3,2},{4,5},{5,4},{6,7},{7,6},{8,9},{9,8},{10,11... | collective-permute-start | bytes 6291464 | tf_op jit(solution)/shard_map/ppermute | solution.py:365
  152.7 3.6 %copy-start.2 = (bf16[2,8,128,128]{2,3,1,0:T(8,128)(2,1)S(1)}, bf16[2,8,128,128]{2,3,1,0:T(8,128)(2,1)}, u32[]{:S(2)}) copy-start(bf16[2,8,128,128]{2,3,1,0:T(8,128)(2,1)} %copy-done.1) | copy-start | bytes 1572868

commit v3 on v1

--- a/solution.py
+++ b/solution.py
@@ -7,6 +7,369 @@
 from jax.experimental import pallas as pl
 from jax.experimental.pallas import tpu as pltpu
 from jax.sharding import PartitionSpec as P
+
+
+MESH = pl.DeviceIdType.MESH
+
+
+def window_kernel(
+    n,
+    pairs,
+    scale,
+    base_ref,
+    ext_ref,
+    first_ref,
+    top_ref,
+    first_pick_ref,
+    top_pick_ref,
+    kept_ref,
+    arrived_ref,
+    vals_ref,
+    held_ref,
+    exts_ref,
+    middle_ref,
+    stack_ref,
+    turned_ref,
+    final_ref,
+    vals_buf,
+    own_sem,
+    send_sem,
+    recv_sem,
+    ext_send,
+    ext_recv,
+    vals_sem,
+    kept_sem,
+    swap_sem,
+):
+    g, k, c = lax.axis_index("grp"), lax.axis_index("path"), lax.axis_index("state")
+    dimension = base_ref.shape[1]
+    variants, selected = top_pick_ref.shape[:2]
+    half_block = top_ref.shape[2]
+    odd = lax.rem(k, 2)
+    pos = (1 - odd) * (k // 2) + odd * (n - 1 - k // 2)
+
+    def place(p):
+        p = lax.rem(p + n, n)
+        high = p // (n // 2)
+        return (1 - high) * (2 * p) + high * (2 * (n - 1 - p) + 1)
+
+    right, left = (g, place(pos + 1), c), (g, place(pos - 1), c)
+    side = lax.rem(g, 2) if pairs else 0
+    partner = (g + 1 - 2 * side, k, c)
+    twin = (g, k, 1 - c)
+
+    barrier = pltpu.get_barrier_semaphore()
+    greeted = [(g, lax.rem(k + d, n), c) for d in range(1, n)] + [twin]
+    if pairs:
+        greeted.append(partner)
+    for other in greeted:
+        pl.semaphore_signal(barrier, inc=1, device_id=other, device_id_type=MESH)
+    pl.semaphore_wait(barrier, len(greeted))
+
+    outer = (dimension + 2) // 3 if pairs else dimension // 2
+    middle = dimension - 2 * outer if pairs else dimension - outer
+
+    def cut(start, length):
+        half = (length + 1) // 2
+        return ((start, half), (start + half, length - half))
+
+    far = dimension - outer
+    runs = (
+        cut(side * far if pairs else 0, outer),
+        cut(outer, middle),
+        cut((1 - side) * far if pairs else 0, outer),
+    )
+
+    started = []
+
+    def start(item):
+        item.start()
+        started.append(item)
+
+    def remote(source, target_ref, send, recv, device):
+        return pltpu.make_async_remote_copy(
+            src_ref=source,
+            dst_ref=target_ref,
+            send_sem=send,
+            recv_sem=recv,
+            device_id=device,
+            device_id_type=MESH,
+        )
+
+    def on_ring(stream, u, step, piece, block, source, target):
+        first, length = runs[stream][piece]
+        ref = held_ref.at[block, u, pl.ds(first, length)]
+        if source is not None:
+            source = source.at[u, pl.ds(first, length)]
+        index = (stream, u, step - 1, piece)
+        return remote(
+            ref if source is None else source, ref, send_sem.at[index], recv_sem.at[index], target
+        )
+
+    def arriving(stream, u, step, piece):
+        block = place(pos + step) if stream == 1 else place(pos - step)
+        return on_ring(stream, u, step, piece, block, None, left)
+
+    def advance(u, step):
+        for piece in range(2):
+            for stream, target in ((0, right), (1, left)):
+                if step > 0:
+                    arriving(stream, u, step, piece).wait_recv()
+                block = place(pos + step) if stream == 1 else place(pos - step)
+                if step < n - 1:
+                    source = base_ref if step == 0 else None
+                    start(on_ring(stream, u, step + 1, piece, block, source, target))
+                if pairs and stream == 0 and step > 0:
+                    first, length = runs[0][piece]
+                    ref = held_ref.at[block, u, pl.ds(first, length)]
+                    index = (2, u, step - 1, piece)
+                    start(remote(ref, ref, send_sem.at[index], recv_sem.at[index], partner))
+
+    def settle(u):
+        if pairs:
+            for step in range(1, n):
+                for piece in range(2):
+                    arriving(2, u, step, piece).wait_recv()
+
+    def choose():
+        for d in range(1, n):
+            block = exts_ref.at[lax.rem(k - d + n, n)]
+            remote(block, block, ext_send.at[d - 1], ext_recv.at[d - 1], twin).wait_recv()
+        codes = []
+        for section in range(2):
+            total = exts_ref[0, selected + section].astype(jnp.float32)
+            for d in range(1, n):
+                total = total + exts_ref[d, selected + section].astype(jnp.float32)
+            codes.append(total)
+        for p in range(n):
+            hits = [
+                [jnp.where(code[p : p + 1] == float(v), 1.0, 0.0) for v in range(variants)]
+                for code in codes
+            ]
+            total = first_ref[0].astype(jnp.float32) * hits[0][0]
+            for v in range(1, variants):
+                total = total + first_ref[v].astype(jnp.float32) * hits[0][v]
+            middle_ref[p] = total.astype(jnp.bfloat16)
+            for part in range(2):
+                total = top_ref[0, part] * hits[1][0]
+                for v in range(1, variants):
+                    total = total + top_ref[v, part] * hits[1][v]
+                stack_ref[pl.ds((part * n + p) * half_block, half_block), :] = total
+        lanes = lax.broadcasted_iota(jnp.int32, (n, dimension), 1)
+        out = jnp.zeros((n, dimension), jnp.float32)
+        for j in range(selected):
+            rows, weights = [], []
+            for picked, code, into in (
+                (top_pick_ref, codes[1], rows),
+                (first_pick_ref, codes[0], weights),
+            ):
+                total = jnp.zeros((n, dimension), jnp.float32)
+                for v in range(variants):
+                    hit = jnp.where(code[:n] == float(v), 1.0, 0.0)
+                    total = total + hit * picked[v, j : j + 1, :]
+                into.append(total)
+            columns = exts_ref[:, j].reshape(dimension, dimension)
+            mixed = jnp.dot(
+                rows[0].astype(jnp.bfloat16), columns, preferred_element_type=jnp.float32
+            )
+            value = jnp.sum(mixed * weights[0], axis=1, keepdims=True)
+            out = jnp.where(lanes == j, value, out)
+        vals_buf[0] = out.astype(jnp.bfloat16).astype(jnp.float32) * scale
+
+    def mix_top(u, low, high):
+        def one(y, carry):
+            block = held_ref[:, u, y].reshape(dimension, dimension)
+            turned_ref[pl.ds(y, dimension, stride=dimension), :] = jnp.dot(
+                stack_ref[...].astype(jnp.bfloat16), block, preferred_element_type=jnp.float32
+            )
+            return carry
+
+        lax.fori_loop(low, high, one, 0, unroll=4)
+
+    def mix_middle(u, low, high):
+        def one(p, carry):
+            matrix = middle_ref[p]
+            for part in range(2):
+                for w in range(half_block):
+                    row = (part * n + p) * half_block + w
+                    begin = pl.multiple_of(row * dimension, dimension)
+                    block = turned_ref[pl.ds(begin, dimension), :].astype(jnp.bfloat16)
+                    final_ref[u, part, p, w] = jnp.dot(
+                        matrix, block, preferred_element_type=jnp.float32
+                    ).astype(jnp.bfloat16)
+            return carry
+
+        lax.fori_loop(low, high, one, 0)
+
+    kept = []
+    quarter = n // 4
+
+    def release(u, q):
+        span = pl.ds(q * quarter, quarter)
+        start(
+            remote(
+                final_ref.at[u, 1, span],
+                arrived_ref.at[u, span],
+                swap_sem.at[0, u, q],
+                swap_sem.at[1, u, q],
+                twin,
+            )
+        )
+        item = pltpu.make_async_copy(
+            final_ref.at[u, 0, span], kept_ref.at[u, span], kept_sem.at[u, q]
+        )
+        item.start()
+        kept.append(item)
+
+    for d in range(1, n):
+        start(
+            remote(
+                ext_ref,
+                exts_ref.at[k],
+                ext_send.at[d - 1],
+                ext_recv.at[d - 1],
+                (g, lax.rem(k + d, n), c),
+            )
+        )
+    own = pltpu.make_async_copy(base_ref, held_ref.at[k], own_sem.at[0])
+    own.start()
+    own_ext = pltpu.make_async_copy(ext_ref, exts_ref.at[k], own_sem.at[1])
+    own_ext.start()
+    advance(0, 0)
+    advance(0, 1)
+    own_ext.wait()
+    choose()
+    own.wait()
+    for step in range(2, n - 1):
+        advance(0, step)
+    start(remote(vals_buf.at[0], vals_buf.at[1], vals_sem.at[0], vals_sem.at[1], twin))
+    advance(1, 0)
+    advance(0, n - 1)
+    settle(0)
+    work = [functools.partial(mix_top, 0, q * dimension // 4, (q + 1) * dimension // 4) for q in range(4)]
+    work += [functools.partial(mix_middle, 0, q * quarter, (q + 1) * quarter) for q in range(4)]
+    for step in range(1, n):
+        advance(1, step)
+        if work:
+            work.pop(0)()
+    while work:
+        work.pop(0)()
+    settle(1)
+    for q in range(4):
+        release(0, q)
+    mix_top(1, 0, dimension)
+    for q in range(4):
+        mix_middle(1, q * quarter, (q + 1) * quarter)
+        if q > 0:
+            release(1, q - 1)
+    remote(
+        vals_buf.at[0], vals_buf.at[1], vals_sem.at[0], vals_sem.at[1], twin
+    ).wait_recv()
+    vals_ref[...] = vals_buf[...]
+    release(1, 3)
+    for u in range(2):
+        for q in range(4):
+            span = pl.ds(q * quarter, quarter)
+            remote(
+                final_ref.at[u, 1, span],
+                arrived_ref.at[u, span],
+                swap_sem.at[0, u, q],
+                swap_sem.at[1, u, q],
+                twin,
+            ).wait_recv()
+    for item in started:
+        item.wait_send()
+    for item in kept:
+        item.wait()
+
+
+def window(base, ext, first, top, first_pick, top_pick, n, scale):
+    pairs = lax.axis_size("grp") % 2 == 0
+    streams = 3 if pairs else 2
+    dimension = base.shape[1]
+    half_block = top.shape[2]
+    state = (2, n, half_block, dimension, dimension)
+    vmem = pl.BlockSpec(memory_space=pltpu.VMEM)
+    hbm = pl.BlockSpec(memory_space=pl.ANY)
+    return pl.pallas_call(
+        functools.partial(window_kernel, n, pairs, scale),
+        out_shape=[
+            jax.ShapeDtypeStruct(state, jnp.bfloat16),
+            jax.ShapeDtypeStruct(state, jnp.bfloat16),
+            jax.ShapeDtypeStruct((2, n, dimension), jnp.float32),
+        ],
+        in_specs=[vmem] * 6,
+        out_specs=[hbm, hbm, vmem],
+        scratch_shapes=[
+            pltpu.VMEM((n,) + base.shape, base.dtype),
+            pltpu.VMEM((n,) + ext.shape, ext.dtype),
+            pltpu.VMEM((n, dimension, dimension), jnp.bfloat16),
+            pltpu.VMEM((dimension, dimension), jnp.float32),
+            pltpu.VMEM((dimension * dimension, dimension), jnp.float32),
+            pltpu.VMEM((2,) + state, jnp.bfloat16),
+            pltpu.VMEM((2, n, dimension), jnp.float32),
+            pltpu.SemaphoreType.DMA((2,)),
+            pltpu.SemaphoreType.DMA((streams, 2, n - 1, 2)),
+            pltpu.SemaphoreType.DMA((streams, 2, n - 1, 2)),
+            pltpu.SemaphoreType.DMA((n - 1,)),
+            pltpu.SemaphoreType.DMA((n - 1,)),
+            pltpu.SemaphoreType.DMA((2,)),
+            pltpu.SemaphoreType.DMA((2, 4)),
+            pltpu.SemaphoreType.DMA((2, 2, 4)),
+        ],
+        compiler_params=pltpu.CompilerParams(
+            collective_id=0, has_side_effects=True, vmem_limit_bytes=52 * 2**20
+        ),
+    )(base, ext, first, top, first_pick, top_pick)
+
+
+def fused_join_kernel(paths, selected, vals_ref, core_ref, kept_ref, arrived_ref, *outs):
+    dimension = kept_ref.shape[-1]
+    step = 32
+    for core in range(2):
+
+        @pl.when(core_ref[0] == core)
+        def _(core=core):
+            for source, out, base in (
+                (kept_ref, outs[core], paths * dimension),
+                (arrived_ref, outs[1 - core], 0),
+            ):
+                for u in range(2):
+
+                    def chunk(i, carry, source=source, out=out, base=base, u=u):
+                        start = pl.multiple_of(i * step, step)
+                        loaded = [
+                            source[u, p, 0, pl.ds(start, step), :].astype(jnp.float32)
+                            for p in range(paths)
+                        ]
+                        for j in range(selected):
+                            total = loaded[0] * vals_ref[base + j]
+                            for p in range(1, paths):
+                                total = total + loaded[p] * vals_ref[base + p * dimension + j]
+                            out[j, 0, u, pl.ds(start, step), :] = total
+                        return carry
+
+                    lax.fori_loop(0, dimension // step, chunk, 0)
+
+
+def fused_join(vals, core, kept, arrived, selected):
+    _, paths, half_block, dimension, _ = kept.shape
+    spec = pl.BlockSpec((2, paths, 1, dimension, dimension), lambda w, *_: (0, 0, w, 0, 0))
+    out_spec = pl.BlockSpec(
+        (selected, 1, 2, dimension, dimension), lambda w, *_: (0, w, 0, 0, 0)
+    )
+    out = jax.ShapeDtypeStruct((selected, half_block, 2, dimension, dimension), jnp.float32)
+    return pl.pallas_call(
+        functools.partial(fused_join_kernel, paths, selected),
+        grid_spec=pltpu.PrefetchScalarGridSpec(
+            num_scalar_prefetch=2,
+            grid=(half_block,),
+            in_specs=[spec] * 2,
+            out_specs=[out_spec] * 2,
+        ),
+        out_shape=[out, out],
+        compiler_params=pltpu.CompilerParams(vmem_limit_bytes=50 * 2**20),
+    )(vals, core, kept, arrived)
 
 
 def mixes(gates, cuts, bits):
@@ -151,6 +514,52 @@
     )(vals, *mine, *other)
 
 
+def body_fused(base, block_gates, cut_ops, path_bits, own_picks):
+    sections = path_bits.shape[1] // 2
+    c, k, owners = lax.axis_index("state"), lax.axis_index("path"), lax.axis_size("path")
+    dimension = base.shape[-1]
+    near = base.shape[2]
+    half_block = near // 2
+    selected = own_picks.shape[0]
+    variants = 2**sections
+    powers = 2 ** jnp.arange(sections, dtype=jnp.int32)
+    every = jnp.arange(variants, dtype=jnp.int32)[:, None] // powers[None, :] % 2
+
+    def of_half(block, cuts):
+        gates = lax.dynamic_index_in_dim(block, c, 0, keepdims=True)
+        ops = lax.dynamic_index_in_dim(cuts, c, 0, keepdims=True)
+        return mixes(gates, ops, every)[:, 0]
+
+    first = of_half(block_gates[1], cut_ops[:, :sections])
+    top = of_half(block_gates[2], cut_ops[:, sections:])
+    top = jnp.transpose(
+        top.reshape(variants, dimension, 2, owners, half_block), (0, 1, 3, 2, 4)
+    ).reshape(variants, dimension, dimension)
+    own_rows = top.reshape(variants, 2, owners, half_block, dimension)
+    own_rows = lax.dynamic_index_in_dim(own_rows, k, 2, keepdims=False)
+    own_rows = jnp.where(c == 1, own_rows[:, ::-1], own_rows).astype(jnp.float32)
+
+    every_lane = jnp.arange(dimension)
+    z_hot = (own_picks[:, None] % dimension == every_lane).astype(jnp.bfloat16)
+    y_hot = (own_picks[:, None] // dimension % dimension == every_lane).astype(jnp.bfloat16)
+    w_hot = (own_picks[:, None] // (dimension * dimension) // 2 == every_lane).astype(jnp.bfloat16)
+    first_pick = jnp.einsum("jy,pyk->pjk", y_hot, first, preferred_element_type=jnp.float32)
+    top_pick = jnp.einsum("jw,pwv->pjv", w_hot, top, preferred_element_type=jnp.float32)
+    lanes = jnp.einsum("jz,uyvz->juvy", z_hot, base, preferred_element_type=jnp.float32)
+    u_own = own_picks // (dimension * dimension) % 2
+    columns = jnp.where(u_own[:, None, None] == 1, lanes[:, 1], lanes[:, 0]).astype(jnp.bfloat16)
+    codes = jnp.sum(path_bits.reshape(2, sections) * powers[None, :], axis=1)
+    spot = jnp.arange(near)[None, :, None] == k
+    marks = jnp.where(spot, codes[:, None, None], 0).astype(jnp.bfloat16)
+    ext = jnp.concatenate([columns, jnp.broadcast_to(marks, (2, near, dimension))], axis=0)
+
+    kept, arrived, vals = window(
+        base, ext, first, own_rows, first_pick, top_pick, owners, 1.0 / math.sqrt(owners)
+    )
+    outs = fused_join(vals.reshape(-1), c[None].astype(jnp.int32), kept, arrived, selected)
+    return tuple(out.reshape(selected, 1, near, dimension, dimension) for out in outs)
+
+
 def body(start_states, block_gates, cut_ops, path_bits, left_pick, right_pick):
     sections = path_bits.shape[1] // 2
     c = lax.axis_index("state")
@@ -173,6 +582,9 @@
 
     picks = jnp.stack([left_pick, right_pick])
     own_picks = lax.dynamic_index_in_dim(picks, c, 0, keepdims=False)
+    if per_device == 1 and owners % 4 == 0 and owners <= 8 and near % 16 == 0:
+        return body_fused(base, block_gates, cut_ops, path_bits, own_picks)
+
     z_hot = (own_picks[:, None] % dimension == jnp.arange(dimension)[None, :]).astype(jnp.bfloat16)
     lanes = jnp.einsum("jz,uyvz->juyv", z_hot, base, preferred_element_type=jnp.float32)
     u_own = own_picks // (dimension * dimension) % 2

time: 221 us -> 136 us (0.62)
  waiting for transfers between devices: 92.9 us -> 0.01 us
  Pallas kernels: 48.5 us -> 107 us
  blocking collectives: 26.9 us -> 0 us
  between operations: 14.5 us -> 0.86 us
  local copies, waits for them, and re-layouts: 21.7 us -> 12.7 us
    all_gather x1 -> x0, waiting for transfers between devices: 91.1 us -> none  [body(): gathered = lax.all_gather(base, 'path', axis=0)]
    pallas_call x3 -> x2, Pallas kernels: 48.5 us -> 107 us  [the longest x1 90.8 us: window(): pl.pallas_call(functools.partial(window_kernel, n, pairs, scale), out_sha...]
    all_gather x1 -> x0, blocking collectives: 26.9 us -> none  [body(): pooled = lax.all_gather(small, ('path', 'state'), axis=0)]
    squeeze x6 -> x0, local copies, waits for them, and re-layouts: 7.09 us -> none  [the longest x2 6.68 us: body(): arrived.append(lax.ppermute(both[1], 'state', [(0, 1), (1, 0)]))]
    another operation x0 -> x2, local copies, waits for them, and re-layouts: none -> 5.94 us  [the longest x1 5.9 us: body_fused(): own_rows = top.reshape(variants, 2, owners, half_block, dimension)]
    reshape x5 -> x1, local copies, waits for them, and re-layouts: 5.04 us -> 0.08 us  [body_fused(): codes = jnp.sum(path_bits.reshape(2, sections) * powers[None, :], axis=1)]
    transpose x2 -> x0, local copies, waits for them, and re-layouts: 3.57 us -> none  [the longest x1 3.56 us: body(): jnp.transpose(columns, (1, 2, 3, 0, 4))]
    dynamic_slice x2, local copies, waits for them, and re-layouts: 0.2 us -> 3.75 us  [body_fused(): own_rows = lax.dynamic_index_in_dim(own_rows, k, 2, keepdims=False)]
  transfers between devices with their start and end apart: 4 -> 1, of which waited for: 2 -> 0; matrix products, arithmetic and copies ran while one was open for 8% -> 5% of each run, Pallas kernels for 0% -> 0%
where the time goes in v3:
time: 136 us; the launch traced here: 133 us
  Pallas kernels  107 us (79%)
  local copies, waits for them, and re-layouts  12.7 us (9%)
  matrix products  5.21 us (4%)
  starting transfers between devices  4.25 us (3%)
  other arithmetic  3.19 us (2%)
    pallas_call x1, Pallas kernels, window(): pl.pallas_call(functools.partial(window_kernel, n, pairs, scale), out_sha...  90.8 us
    pallas_call x1, Pallas kernels, fused_join(): pl.pallas_call(functools.partial(fused_join_kernel, paths, selected), gri...  16 us
    another operation x1, local copies, waits for them, and re-layouts, body_fused(): own_rows = top.reshape(variants, 2, owners, half_block, dimension)  5.9 us
    all_to_all x1, starting transfers between devices, body(): lax.all_to_all(start_states, 'state', split_axis=0, concat_axis=1, tiled=...  4.25 us
    dynamic_slice x2, local copies, waits for them, and re-layouts, body_fused(): own_rows = lax.dynamic_index_in_dim(own_rows, k, 2, keepdims=False)  3.75 us
  transfers between devices with their start and end apart: 1, of which 0 were waited for; matrix products, arithmetic and copies ran while one was open for 5% of the time, Pallas kernels for 0%

profile of v3, /device:TPU:9, one launch (start us, length us, event | category | flops | bytes accessed | tf_op | source)
XLA Modules:
  0.0 133.0 jit_solution(3281405682293384426)
XLA Ops:
  0.6 4.3 %all-to-all-start = ((bf16[2,1,16,128,128]{4,3,2,1,0:T(8,128)(2,1)}), bf16[2,1,16,128,128]{4,3,2,1,0:T(8,128)(2,1)S(1)}, u32[]{:S(2)}, u32[]{:S(2)}) async-start(bf16[2,1,16,128,128]{4,3,2,1,0:T(8,128)(2,1)} %param.6), calls=%async_computation | async-start | bytes 2097152 | tf_op jit(solution)/shard_map/all_to_all | solution.py:575
  5.0 0.5 broadcast.1172
  5.5 1.3 reduce.27
  6.8 0.1 reshape.600
  6.9 0.7 pad_add_fusion
  7.7 0.1 multiply_reduce_fusion
  7.8 0.2 add_select_fusion.6
  8.0 0.8 fusion.128
  8.8 0.2 fusion.105
  9.0 0.1 broadcast_select_fusion.4
  9.1 0.1 broadcast_select_fusion
  9.2 0.1 broadcast_select_fusion.2
  9.3 0.9 fusion.127
  10.2 0.1 fusion.67
  10.4 0.1 fusion.65
  10.5 0.1 fusion.81
  10.6 0.7 convolution_convert_fusion.1
  11.4 0.0 all-to-all-done
  11.5 0.7 fusion.base_ref
  12.2 2.6 %fusion.95 = bf16[2,128,16,8]{2,3,1,0:T(8,128)(2,1)S(1)} fusion(bf16[2,128,16,128]{3,2,1,0:T(8,128)(2,1)S(1)} %fusion.base_ref, s32[8]{0:T(128)S(1)} %and_select_fusion.3), kind=kOutput, calls=%fused_computation.146 | convolution fusion | flops 8389632 | bytes 1114144 | tf_op jit(solution)/shard_map/jz,uyvz->juvy/dot_general | solution.py:548
  14.8 0.3 copy.19
  15.1 5.9 %reshape_reshape.3 = bf16[8,2,8,8,128]{3,2,1,4,0:T(8,128)(2,1)} reshape(bf16[8,128,8,2,8]{1,4,3,2,0:T(8,128)(2,1)S(1)} %bitcast.149) | data formatting | bytes 524288 | tf_op jit(solution)/shard_map/reshape;reshape | solution.py:538
  21.0 3.3 %constant_dynamic-slice_fusion.10 = bf16[8,2,1,8,128]{3,2,1,4,0:T(2,128)(2,1)S(1)} fusion(bf16[8,2,8,8,128]{3,2,1,4,0:T(8,128)(2,1)} %reshape_reshape.3, s32[]{:T(128)S(6)} %select_n.631), kind=kLoop, calls=%fused_computation.135 | loop fusion | bytes 65540 | tf_op jit(solution)/shard_map/jit(dynamic_index_in_dim)/dynamic_slice | solution.py:539
  24.3 0.5 copy.22
  24.8 0.1 select_convert_fusion
  24.8 0.8 fusion.1.first_ref
  25.6 0.2 convolution_bitcast_fusion.1.first_pick_ref
  25.8 0.2 convolution_bitcast_fusion.top_pick_ref
  26.0 0.1 fusion.76
  26.1 0.1 broadcast_in_dim.427
  26.2 90.8 %shard_map.77 = (bf16[2,8,8,128,128]{4,3,2,1,0:T(8,128)(2,1)}, bf16[2,8,8,128,128]{4,3,2,1,0:T(8,128)(2,1)}, f32[2,8,128]{2,1,0:T(8,128)S(1)}) custom-call(bf16[2,128,16,128]{3,2,1,0:T(8,128)(2,1)S(1)} %fusion.base_ref, bf16[10,16,128]{2,1,0:T(8,128)(2,1)S(1)} %pad_maximum_fusion.ext_ref, bf16[8,128,128]{2,1,0:T(8,128)(2,1)S(1)} %fusion.1.first_ref, ...), custom_call_target="tpu_custom_call" | custom-call | tf_op jit(solution)/shard_map/pallas_call | solution.py:294
  117.0 16.0 %shard_map.78 = (f32[8,8,2,128,128]{4,3,2,1,0:T(8,128)}, f32[8,8,2,128,128]{4,3,2,1,0:T(8,128)}) custom-call(f32[2048]{0:T(1024)S(1)} %bitcast.147, s32[1]{0:T(128)} %bitcast.63.core_ref, bf16[2,8,8,128,128]{4,3,2,1,0:T(8,128)(2,1)} %get-tuple-element.8.kept_ref, bf16[2,8,8,128,128]{4,3,2,1,0:T(8,128)(2,1)} %get-tuple-element.9.arrived_ref), custom_call_target="tpu_custom_call" | custom-call | tf_op jit(solution)/shard_map/pallas_call | solution.py:362
  (22 shorter events, 0.2 us)
Async XLA Ops:
  0.6 10.8 %all-to-all-start = ((bf16[2,1,16,128,128]{4,3,2,1,0:T(8,128)(2,1)}), bf16[2,1,16,128,128]{4,3,2,1,0:T(8,128)(2,1)S(1)}, u32[]{:S(2)}, u32[]{:S(2)}) async-start(bf16[2,1,16,128,128]{4,3,2,1,0:T(8,128)(2,1)} %param.6), calls=%async_computation | async-start | bytes 2097152 | tf_op jit(solution)/shard_map/all_to_all | solution.py:575

commit v4 on v3

--- a/solution.py
+++ b/solution.py
@@ -16,12 +16,11 @@
     n,
     pairs,
     scale,
+    half_block,
     base_ref,
     ext_ref,
     first_ref,
     top_ref,
-    first_pick_ref,
-    top_pick_ref,
     kept_ref,
     arrived_ref,
     vals_ref,
@@ -29,6 +28,7 @@
     exts_ref,
     middle_ref,
     stack_ref,
+    packed_ref,
     turned_ref,
     final_ref,
     vals_buf,
@@ -43,8 +43,8 @@
 ):
     g, k, c = lax.axis_index("grp"), lax.axis_index("path"), lax.axis_index("state")
     dimension = base_ref.shape[1]
-    variants, selected = top_pick_ref.shape[:2]
-    half_block = top_ref.shape[2]
+    variants = top_ref.shape[0]
+    selected = top_ref.shape[1] - 2 * half_block
     odd = lax.rem(k, 2)
     pos = (1 - odd) * (k // 2) + odd * (n - 1 - k // 2)
 
@@ -110,8 +110,12 @@
         block = place(pos + step) if stream == 1 else place(pos - step)
         return on_ring(stream, u, step, piece, block, None, left)
 
+    work = []
+
     def advance(u, step):
         for piece in range(2):
+            if work and u == 1:
+                work.pop(0)()
             for stream, target in ((0, right), (1, left)):
                 if step > 0:
                     arriving(stream, u, step, piece).wait_recv()
@@ -146,27 +150,29 @@
                 [jnp.where(code[p : p + 1] == float(v), 1.0, 0.0) for v in range(variants)]
                 for code in codes
             ]
-            total = first_ref[0].astype(jnp.float32) * hits[0][0]
+            total = first_ref[0, :dimension] * hits[0][0]
             for v in range(1, variants):
-                total = total + first_ref[v].astype(jnp.float32) * hits[0][v]
+                total = total + first_ref[v, :dimension] * hits[0][v]
             middle_ref[p] = total.astype(jnp.bfloat16)
             for part in range(2):
-                total = top_ref[0, part] * hits[1][0]
+                span = slice(part * half_block, (part + 1) * half_block)
+                total = top_ref[0, span] * hits[1][0]
                 for v in range(1, variants):
-                    total = total + top_ref[v, part] * hits[1][v]
+                    total = total + top_ref[v, span] * hits[1][v]
                 stack_ref[pl.ds((part * n + p) * half_block, half_block), :] = total
+        packed_ref[...] = stack_ref[...].astype(jnp.bfloat16)
         lanes = lax.broadcasted_iota(jnp.int32, (n, dimension), 1)
         out = jnp.zeros((n, dimension), jnp.float32)
         for j in range(selected):
             rows, weights = [], []
-            for picked, code, into in (
-                (top_pick_ref, codes[1], rows),
-                (first_pick_ref, codes[0], weights),
+            for picked, at, code, into in (
+                (top_ref, 2 * half_block + j, codes[1], rows),
+                (first_ref, dimension + j, codes[0], weights),
             ):
                 total = jnp.zeros((n, dimension), jnp.float32)
                 for v in range(variants):
                     hit = jnp.where(code[:n] == float(v), 1.0, 0.0)
-                    total = total + hit * picked[v, j : j + 1, :]
+                    total = total + hit * picked[v, at : at + 1, :]
                 into.append(total)
             columns = exts_ref[:, j].reshape(dimension, dimension)
             mixed = jnp.dot(
@@ -177,26 +183,39 @@
         vals_buf[0] = out.astype(jnp.bfloat16).astype(jnp.float32) * scale
 
     def mix_top(u, low, high):
-        def one(y, carry):
-            block = held_ref[:, u, y].reshape(dimension, dimension)
-            turned_ref[pl.ds(y, dimension, stride=dimension), :] = jnp.dot(
-                stack_ref[...].astype(jnp.bfloat16), block, preferred_element_type=jnp.float32
+        def one(i, carry):
+            blocks = [held_ref[:, u, 2 * i + e].reshape(dimension, dimension) for e in range(2)]
+            mixed = jnp.dot(
+                packed_ref[...],
+                jnp.concatenate(blocks, axis=1),
+                preferred_element_type=jnp.float32,
             )
+            for e in range(2):
+                turned_ref[pl.ds(2 * i + e, dimension, stride=dimension), :] = mixed[
+                    :, e * dimension : (e + 1) * dimension
+                ]
             return carry
 
-        lax.fori_loop(low, high, one, 0, unroll=4)
+        lax.fori_loop(low // 2, high // 2, one, 0, unroll=2)
 
     def mix_middle(u, low, high):
         def one(p, carry):
             matrix = middle_ref[p]
             for part in range(2):
-                for w in range(half_block):
+                for w in range(0, half_block, 2):
                     row = (part * n + p) * half_block + w
                     begin = pl.multiple_of(row * dimension, dimension)
-                    block = turned_ref[pl.ds(begin, dimension), :].astype(jnp.bfloat16)
-                    final_ref[u, part, p, w] = jnp.dot(
-                        matrix, block, preferred_element_type=jnp.float32
+                    blocks = [
+                        turned_ref[pl.ds(begin + e * dimension, dimension), :].astype(jnp.bfloat16)
+                        for e in range(2)
+                    ]
+                    mixed = jnp.dot(
+                        matrix,
+                        jnp.concatenate(blocks, axis=1),
+                        preferred_element_type=jnp.float32,
                     ).astype(jnp.bfloat16)
+                    for e in range(2):
+                        final_ref[u, part, p, w + e] = mixed[:, e * dimension : (e + 1) * dimension]
             return carry
 
         lax.fori_loop(low, high, one, 0)
@@ -246,12 +265,12 @@
     advance(1, 0)
     advance(0, n - 1)
     settle(0)
-    work = [functools.partial(mix_top, 0, q * dimension // 4, (q + 1) * dimension // 4) for q in range(4)]
-    work += [functools.partial(mix_middle, 0, q * quarter, (q + 1) * quarter) for q in range(4)]
+    for q in range(8):
+        work.append(functools.partial(mix_top, 0, q * dimension // 8, (q + 1) * dimension // 8))
+    for q in range(n):
+        work.append(functools.partial(mix_middle, 0, q, q + 1))
     for step in range(1, n):
         advance(1, step)
-        if work:
-            work.pop(0)()
     while work:
         work.pop(0)()
     settle(1)
@@ -283,28 +302,28 @@
         item.wait()
 
 
-def window(base, ext, first, top, first_pick, top_pick, n, scale):
+def window(base, ext, first, top, half_block, n, scale):
     pairs = lax.axis_size("grp") % 2 == 0
     streams = 3 if pairs else 2
     dimension = base.shape[1]
-    half_block = top.shape[2]
     state = (2, n, half_block, dimension, dimension)
     vmem = pl.BlockSpec(memory_space=pltpu.VMEM)
     hbm = pl.BlockSpec(memory_space=pl.ANY)
     return pl.pallas_call(
-        functools.partial(window_kernel, n, pairs, scale),
+        functools.partial(window_kernel, n, pairs, scale, half_block),
         out_shape=[
             jax.ShapeDtypeStruct(state, jnp.bfloat16),
             jax.ShapeDtypeStruct(state, jnp.bfloat16),
             jax.ShapeDtypeStruct((2, n, dimension), jnp.float32),
         ],
-        in_specs=[vmem] * 6,
+        in_specs=[vmem] * 4,
         out_specs=[hbm, hbm, vmem],
         scratch_shapes=[
             pltpu.VMEM((n,) + base.shape, base.dtype),
             pltpu.VMEM((n,) + ext.shape, ext.dtype),
             pltpu.VMEM((n, dimension, dimension), jnp.bfloat16),
             pltpu.VMEM((dimension, dimension), jnp.float32),
+            pltpu.VMEM((dimension, dimension), jnp.bfloat16),
             pltpu.VMEM((dimension * dimension, dimension), jnp.float32),
             pltpu.VMEM((2,) + state, jnp.bfloat16),
             pltpu.VMEM((2, n, dimension), jnp.float32),
@@ -320,7 +339,7 @@
         compiler_params=pltpu.CompilerParams(
             collective_id=0, has_side_effects=True, vmem_limit_bytes=52 * 2**20
         ),
-    )(base, ext, first, top, first_pick, top_pick)
+    )(base, ext, first, top)
 
 
 def fused_join_kernel(paths, selected, vals_ref, core_ref, kept_ref, arrived_ref, *outs):
@@ -372,11 +391,13 @@
     )(vals, core, kept, arrived)
 
 
-def mixes(gates, cuts, bits):
+def mixes(gates, cuts, bits, columns=None):
     dimension = gates.shape[-1]
     count = bits.shape[1]
     rows = lax.broadcasted_iota(jnp.int32, (dimension, dimension), 0)
     cols = lax.broadcasted_iota(jnp.int32, (dimension, dimension), 1)
+    if columns is not None:
+        cols = columns(cols)
     block = 2**count
     kernel = jnp.where(rows // block == cols // block, 1.0, 0.0).astype(jnp.float32)
     for k in reversed(range(count)):
@@ -525,26 +546,33 @@
     powers = 2 ** jnp.arange(sections, dtype=jnp.int32)
     every = jnp.arange(variants, dtype=jnp.int32)[:, None] // powers[None, :] % 2
 
-    def of_half(block, cuts):
-        gates = lax.dynamic_index_in_dim(block, c, 0, keepdims=True)
-        ops = lax.dynamic_index_in_dim(cuts, c, 0, keepdims=True)
-        return mixes(gates, ops, every)[:, 0]
-
-    first = of_half(block_gates[1], cut_ops[:, :sections])
-    top = of_half(block_gates[2], cut_ops[:, sections:])
-    top = jnp.transpose(
-        top.reshape(variants, dimension, 2, owners, half_block), (0, 1, 3, 2, 4)
-    ).reshape(variants, dimension, dimension)
-    own_rows = top.reshape(variants, 2, owners, half_block, dimension)
-    own_rows = lax.dynamic_index_in_dim(own_rows, k, 2, keepdims=False)
-    own_rows = jnp.where(c == 1, own_rows[:, ::-1], own_rows).astype(jnp.float32)
+    def of_half(array):
+        return lax.dynamic_index_in_dim(array, c, 0, keepdims=False)
 
     every_lane = jnp.arange(dimension)
     z_hot = (own_picks[:, None] % dimension == every_lane).astype(jnp.bfloat16)
     y_hot = (own_picks[:, None] // dimension % dimension == every_lane).astype(jnp.bfloat16)
     w_hot = (own_picks[:, None] // (dimension * dimension) // 2 == every_lane).astype(jnp.bfloat16)
-    first_pick = jnp.einsum("jy,pyk->pjk", y_hot, first, preferred_element_type=jnp.float32)
-    top_pick = jnp.einsum("jw,pwv->pjv", w_hot, top, preferred_element_type=jnp.float32)
+    second, third = of_half(block_gates[1]), of_half(block_gates[2])
+    ops = of_half(cut_ops)
+
+    def picked(hot, gate):
+        return jnp.dot(hot, gate, preferred_element_type=jnp.float32).astype(jnp.bfloat16)
+
+    first = mixes(
+        jnp.concatenate([second, picked(y_hot, second)])[None], ops[None, :sections], every
+    )[:, 0].astype(jnp.float32)
+
+    def columns_of(q):
+        return q // half_block % 2 * (dimension // 2) + q // near * half_block + q % half_block
+
+    rows = third.reshape(2, owners, half_block, dimension)
+    rows = lax.dynamic_index_in_dim(rows, k, 1, keepdims=False)
+    rows = jnp.where(c == 1, rows[::-1], rows).reshape(near, dimension)
+    top = mixes(
+        jnp.concatenate([rows, picked(w_hot, third)])[None], ops[None, sections:], every, columns_of
+    )[:, 0].astype(jnp.float32)
+
     lanes = jnp.einsum("jz,uyvz->juvy", z_hot, base, preferred_element_type=jnp.float32)
     u_own = own_picks // (dimension * dimension) % 2
     columns = jnp.where(u_own[:, None, None] == 1, lanes[:, 1], lanes[:, 0]).astype(jnp.bfloat16)
@@ -554,7 +582,7 @@
     ext = jnp.concatenate([columns, jnp.broadcast_to(marks, (2, near, dimension))], axis=0)
 
     kept, arrived, vals = window(
-        base, ext, first, own_rows, first_pick, top_pick, owners, 1.0 / math.sqrt(owners)
+        base, ext, first, top, half_block, owners, 1.0 / math.sqrt(owners)
     )
     outs = fused_join(vals.reshape(-1), c[None].astype(jnp.int32), kept, arrived, selected)
     return tuple(out.reshape(selected, 1, near, dimension, dimension) for out in outs)

time: 136 us -> 126 us (0.926)
  local copies, waits for them, and re-layouts: 12.7 us -> 3.12 us
    another operation x2 -> x0, local copies, waits for them, and re-layouts: 5.94 us -> none  [the longest x1 5.9 us: body_fused(): own_rows = top.reshape(variants, 2, owners, half_block, dimension)]
    dynamic_slice x2 -> x1, local copies, waits for them, and re-layouts: 3.75 us -> 0.01 us  [of_half(): return lax.dynamic_index_in_dim(array, c, 0, keepdims=False)]
  transfers between devices with their start and end apart: 1 -> 1, of which waited for: 0 -> 0; matrix products, arithmetic and copies ran while one was open for 5% -> 4% of each run, Pallas kernels for 0% -> 0%
where the time goes in v4:
time: 126 us; the launch traced here: 124 us
  Pallas kernels  107 us (85%)
  matrix products  5.12 us (4%)
  starting transfers between devices  4.25 us (3%)
  other arithmetic  3.26 us (3%)
  local copies, waits for them, and re-layouts  3.12 us (2%)
    pallas_call x1, Pallas kernels, window(): pl.pallas_call(functools.partial(window_kernel, n, pairs, scale, half_blo...  91.5 us
    pallas_call x1, Pallas kernels, fused_join(): pl.pallas_call(functools.partial(fused_join_kernel, paths, selected), gri...  16 us
    all_to_all x1, starting transfers between devices, body(): lax.all_to_all(start_states, 'state', split_axis=0, concat_axis=1, tiled=...  4.25 us
    dot_general x1, matrix products, body_fused(): jnp.einsum('jz,uyvz->juvy', z_hot, base, preferred_element_type=jnp.float32)  2.56 us
  transfers between devices with their start and end apart: 1, of which 0 were waited for; matrix products, arithmetic and copies ran while one was open for 4% of the time, Pallas kernels for 0%

profile of v4, /device:TPU:9, one launch (start us, length us, event | category | flops | bytes accessed | tf_op | source)
XLA Modules:
  0.0 124.1 jit_solution(14178983351870613611)
XLA Ops:
  0.6 4.3 %all-to-all-start = ((bf16[2,1,16,128,128]{4,3,2,1,0:T(8,128)(2,1)}), bf16[2,1,16,128,128]{4,3,2,1,0:T(8,128)(2,1)S(1)}, u32[]{:S(2)}, u32[]{:S(2)}) async-start(bf16[2,1,16,128,128]{4,3,2,1,0:T(8,128)(2,1)} %param.6), calls=%async_computation | async-start | bytes 2097152 | tf_op jit(solution)/shard_map/all_to_all | solution.py:603
  5.1 0.1 fusion.102
  5.2 0.5 broadcast.1462
  5.7 1.3 %reduce.27 = s32[6]{0:T(128)S(1)} reduce(s32[1,6]{1,0:T(1,128)} %param.9, s32[]{:T(128)} %broadcast.1462), dimensions={0}, to_apply=%param.9.reduce_sub_computation.3 | reduce | bytes 52 | tf_op args[3]
  7.0 0.1 reshape.813
  7.1 0.7 pad_add_fusion
  7.9 0.1 multiply_reduce_fusion
  8.0 0.2 add_select_fusion.13
  8.2 1.1 fusion.129
  9.3 0.1 broadcast_select_fusion.4
  9.4 0.1 broadcast_select_fusion
  9.5 0.1 broadcast_select_fusion.2
  9.6 0.9 fusion.144
  10.6 0.0 all-to-all-done
  10.6 0.7 fusion.base_ref
  11.4 2.6 %fusion.115 = bf16[2,128,16,8]{2,3,1,0:T(8,128)(2,1)S(1)} fusion(bf16[2,128,16,128]{3,2,1,0:T(8,128)(2,1)S(1)} %fusion.base_ref, s32[8]{0:T(128)S(1)} %and_select_fusion.3), kind=kOutput, calls=%fused_computation.194 | convolution fusion | flops 8389632 | bytes 1114144 | tf_op jit(solution)/shard_map/jz,uyvz->juvy/dot_general | solution.py:576
  13.9 0.3 copy.17
  14.3 0.1 select_convert_fusion
  14.3 0.2 convolution_convert_fusion.4
  14.5 0.2 convolution_convert_fusion.3
  14.7 0.1 fusion.92
  14.8 0.1 broadcast_in_dim.431
  14.9 0.1 fusion.72
  15.0 0.1 fusion.70
  15.1 0.8 fusion.3.first_ref
  15.9 0.7 fusion.6.top_ref
  16.6 91.5 %shard_map.77 = (bf16[2,8,8,128,128]{4,3,2,1,0:T(8,128)(2,1)}, bf16[2,8,8,128,128]{4,3,2,1,0:T(8,128)(2,1)}, f32[2,8,128]{2,1,0:T(8,128)S(1)}) custom-call(bf16[2,128,16,128]{3,2,1,0:T(8,128)(2,1)S(1)} %fusion.base_ref, bf16[10,16,128]{2,1,0:T(8,128)(2,1)S(1)} %pad_maximum_fusion.ext_ref, f32[8,136,128]{2,1,0:T(8,128)S(1)} %fusion.3.first_ref, ...), custom_call_target="tpu_custom_call" | custom-call | tf_op jit(solution)/shard_map/pallas_call | solution.py:312
  108.1 16.0 %shard_map.78 = (f32[8,8,2,128,128]{4,3,2,1,0:T(8,128)}, f32[8,8,2,128,128]{4,3,2,1,0:T(8,128)}) custom-call(f32[2048]{0:T(1024)S(1)} %bitcast.144, s32[1]{0:T(128)} %bitcast.57.core_ref, bf16[2,8,8,128,128]{4,3,2,1,0:T(8,128)(2,1)} %get-tuple-element.8.kept_ref, bf16[2,8,8,128,128]{4,3,2,1,0:T(8,128)(2,1)} %get-tuple-element.9.arrived_ref), custom_call_target="tpu_custom_call" | custom-call | tf_op jit(solution)/shard_map/pallas_call | solution.py:381
  (28 shorter events, 0.3 us)
Async XLA Ops:
  0.6 10.0 %all-to-all-start = ((bf16[2,1,16,128,128]{4,3,2,1,0:T(8,128)(2,1)}), bf16[2,1,16,128,128]{4,3,2,1,0:T(8,128)(2,1)S(1)}, u32[]{:S(2)}, u32[]{:S(2)}) async-start(bf16[2,1,16,128,128]{4,3,2,1,0:T(8,128)(2,1)} %param.6), calls=%async_computation | async-start | bytes 2097152 | tf_op jit(solution)/shard_map/all_to_all | solution.py:603

commit v5 on v4

--- a/solution.py
+++ b/solution.py
@@ -114,7 +114,7 @@
 
     def advance(u, step):
         for piece in range(2):
-            if work and u == 1:
+            if work:
                 work.pop(0)()
             for stream, target in ((0, right), (1, left)):
                 if step > 0:
@@ -145,7 +145,7 @@
             for d in range(1, n):
                 total = total + exts_ref[d, selected + section].astype(jnp.float32)
             codes.append(total)
-        for p in range(n):
+        def select(p):
             hits = [
                 [jnp.where(code[p : p + 1] == float(v), 1.0, 0.0) for v in range(variants)]
                 for code in codes
@@ -160,27 +160,31 @@
                 for v in range(1, variants):
                     total = total + top_ref[v, span] * hits[1][v]
                 stack_ref[pl.ds((part * n + p) * half_block, half_block), :] = total
-        packed_ref[...] = stack_ref[...].astype(jnp.bfloat16)
-        lanes = lax.broadcasted_iota(jnp.int32, (n, dimension), 1)
-        out = jnp.zeros((n, dimension), jnp.float32)
-        for j in range(selected):
-            rows, weights = [], []
-            for picked, at, code, into in (
-                (top_ref, 2 * half_block + j, codes[1], rows),
-                (first_ref, dimension + j, codes[0], weights),
-            ):
-                total = jnp.zeros((n, dimension), jnp.float32)
-                for v in range(variants):
-                    hit = jnp.where(code[:n] == float(v), 1.0, 0.0)
-                    total = total + hit * picked[v, at : at + 1, :]
-                into.append(total)
-            columns = exts_ref[:, j].reshape(dimension, dimension)
-            mixed = jnp.dot(
-                rows[0].astype(jnp.bfloat16), columns, preferred_element_type=jnp.float32
-            )
-            value = jnp.sum(mixed * weights[0], axis=1, keepdims=True)
-            out = jnp.where(lanes == j, value, out)
-        vals_buf[0] = out.astype(jnp.bfloat16).astype(jnp.float32) * scale
+
+        def values():
+            packed_ref[...] = stack_ref[...].astype(jnp.bfloat16)
+            lanes = lax.broadcasted_iota(jnp.int32, (n, dimension), 1)
+            out = jnp.zeros((n, dimension), jnp.float32)
+            for j in range(selected):
+                rows, weights = [], []
+                for picked, at, code, into in (
+                    (top_ref, 2 * half_block + j, codes[1], rows),
+                    (first_ref, dimension + j, codes[0], weights),
+                ):
+                    total = jnp.zeros((n, dimension), jnp.float32)
+                    for v in range(variants):
+                        hit = jnp.where(code[:n] == float(v), 1.0, 0.0)
+                        total = total + hit * picked[v, at : at + 1, :]
+                    into.append(total)
+                columns = exts_ref[:, j].reshape(dimension, dimension)
+                mixed = jnp.dot(
+                    rows[0].astype(jnp.bfloat16), columns, preferred_element_type=jnp.float32
+                )
+                value = jnp.sum(mixed * weights[0], axis=1, keepdims=True)
+                out = jnp.where(lanes == j, value, out)
+            vals_buf[0] = out.astype(jnp.bfloat16).astype(jnp.float32) * scale
+
+        return [functools.partial(select, p) for p in range(n)] + [values]
 
     def mix_top(u, low, high):
         def one(i, carry):
@@ -257,14 +261,16 @@
     advance(0, 0)
     advance(0, 1)
     own_ext.wait()
-    choose()
     own.wait()
+    work.extend(choose())
     for step in range(2, n - 1):
         advance(0, step)
-    start(remote(vals_buf.at[0], vals_buf.at[1], vals_sem.at[0], vals_sem.at[1], twin))
+    while work:
+        work.pop(0)()
     advance(1, 0)
     advance(0, n - 1)
     settle(0)
+    start(remote(vals_buf.at[0], vals_buf.at[1], vals_sem.at[0], vals_sem.at[1], twin))
     for q in range(8):
         work.append(functools.partial(mix_top, 0, q * dimension // 8, (q + 1) * dimension // 8))
     for q in range(n):

time: 126 us -> 126 us (level)
  no operation moved by 1% of the time
where the time goes in v5:
time: 126 us; the launch traced here: 124 us
  Pallas kernels  107 us (85%)
  matrix products  5.12 us (4%)
  starting transfers between devices  4.25 us (3%)
  other arithmetic  3.26 us (3%)
  local copies, waits for them, and re-layouts  3.12 us (2%)
    pallas_call x1, Pallas kernels, window(): pl.pallas_call(functools.partial(window_kernel, n, pairs, scale, half_blo...  91.5 us
    pallas_call x1, Pallas kernels, fused_join(): pl.pallas_call(functools.partial(fused_join_kernel, paths, selected), gri...  16 us
    all_to_all x1, starting transfers between devices, body(): lax.all_to_all(start_states, 'state', split_axis=0, concat_axis=1, tiled=...  4.25 us
    dot_general x1, matrix products, body_fused(): jnp.einsum('jz,uyvz->juvy', z_hot, base, preferred_element_type=jnp.float32)  2.56 us
  transfers between devices with their start and end apart: 1, of which 0 were waited for; matrix products, arithmetic and copies ran while one was open for 4% of the time, Pallas kernels for 0%

profile of v5, /device:TPU:9, one launch (start us, length us, event | category | flops | bytes accessed | tf_op | source)
XLA Modules:
  0.0 124.1 jit_solution(2394345812735194463)
XLA Ops:
  0.6 4.3 %all-to-all-start = ((bf16[2,1,16,128,128]{4,3,2,1,0:T(8,128)(2,1)}), bf16[2,1,16,128,128]{4,3,2,1,0:T(8,128)(2,1)S(1)}, u32[]{:S(2)}, u32[]{:S(2)}) async-start(bf16[2,1,16,128,128]{4,3,2,1,0:T(8,128)(2,1)} %param.6), calls=%async_computation | async-start | bytes 2097152 | tf_op jit(solution)/shard_map/all_to_all | solution.py:609
  5.1 0.1 fusion.102
  5.2 0.5 broadcast.1462
  5.7 1.3 %reduce.27 = s32[6]{0:T(128)S(1)} reduce(s32[1,6]{1,0:T(1,128)} %param.9, s32[]{:T(128)} %broadcast.1462), dimensions={0}, to_apply=%param.9.reduce_sub_computation.3 | reduce | bytes 52 | tf_op args[3]
  7.0 0.1 reshape.813
  7.1 0.7 pad_add_fusion
  7.9 0.1 multiply_reduce_fusion
  8.0 0.2 add_select_fusion.13
  8.2 1.1 fusion.129
  9.3 0.1 broadcast_select_fusion.4
  9.4 0.1 broadcast_select_fusion
  9.5 0.1 broadcast_select_fusion.2
  9.6 0.9 fusion.144
  10.6 0.0 all-to-all-done
  10.6 0.7 fusion.base_ref
  11.4 2.6 %fusion.115 = bf16[2,128,16,8]{2,3,1,0:T(8,128)(2,1)S(1)} fusion(bf16[2,128,16,128]{3,2,1,0:T(8,128)(2,1)S(1)} %fusion.base_ref, s32[8]{0:T(128)S(1)} %and_select_fusion.3), kind=kOutput, calls=%fused_computation.194 | convolution fusion | flops 8389632 | bytes 1114144 | tf_op jit(solution)/shard_map/jz,uyvz->juvy/dot_general | solution.py:582
  13.9 0.3 copy.17
  14.3 0.1 select_convert_fusion
  14.3 0.2 convolution_convert_fusion.4
  14.5 0.2 convolution_convert_fusion.3
  14.7 0.1 fusion.92
  14.8 0.1 broadcast_in_dim.431
  14.9 0.1 fusion.72
  15.0 0.1 fusion.70
  15.1 0.8 fusion.3.first_ref
  15.9 0.7 fusion.6.top_ref
  16.6 91.5 %shard_map.77 = (bf16[2,8,8,128,128]{4,3,2,1,0:T(8,128)(2,1)}, bf16[2,8,8,128,128]{4,3,2,1,0:T(8,128)(2,1)}, f32[2,8,128]{2,1,0:T(8,128)S(1)}) custom-call(bf16[2,128,16,128]{3,2,1,0:T(8,128)(2,1)S(1)} %fusion.base_ref, bf16[10,16,128]{2,1,0:T(8,128)(2,1)S(1)} %pad_maximum_fusion.ext_ref, f32[8,136,128]{2,1,0:T(8,128)S(1)} %fusion.3.first_ref, ...), custom_call_target="tpu_custom_call" | custom-call | tf_op jit(solution)/shard_map/pallas_call | solution.py:318
  108.1 16.0 %shard_map.78 = (f32[8,8,2,128,128]{4,3,2,1,0:T(8,128)}, f32[8,8,2,128,128]{4,3,2,1,0:T(8,128)}) custom-call(f32[2048]{0:T(1024)S(1)} %bitcast.144, s32[1]{0:T(128)} %bitcast.57.core_ref, bf16[2,8,8,128,128]{4,3,2,1,0:T(8,128)(2,1)} %get-tuple-element.8.kept_ref, bf16[2,8,8,128,128]{4,3,2,1,0:T(8,128)(2,1)} %get-tuple-element.9.arrived_ref), custom_call_target="tpu_custom_call" | custom-call | tf_op jit(solution)/shard_map/pallas_call | solution.py:387
  (28 shorter events, 0.3 us)
Async XLA Ops:
  0.6 10.0 %all-to-all-start = ((bf16[2,1,16,128,128]{4,3,2,1,0:T(8,128)(2,1)}), bf16[2,1,16,128,128]{4,3,2,1,0:T(8,128)(2,1)S(1)}, u32[]{:S(2)}, u32[]{:S(2)}) async-start(bf16[2,1,16,128,128]{4,3,2,1,0:T(8,128)(2,1)} %param.6), calls=%async_computation | async-start | bytes 2097152 | tf_op jit(solution)/shard_map/all_to_all | solution.py:609
